TPU v7x, 32 devices: a whole 2x2x4 slice. The times are simulated.
32 devices in a mesh: lon: 8 (over y, x, core), lat: 4 (over z).
Axes of the slice: x: 2, y: 2, z: 4, core: 2. Of those that a mesh axis runs over, the one named last changes fastest.
Arguments:
- u_wind: float32 [256, 192, 1024], P(None, 'lat', 'lon'), may hold values from -40 to 40
- v_wind: float32 [256, 192, 1024], P(None, 'lat', 'lon'), may hold values from -40 to 40
Outputs:
- eof_basis: float32 [256, 2, 192, 1024], P(None, None, 'lat', 'lon')
- r_factor: float32 [256, 256], replicated
All inputs are finite; a program needn't handle non-finite values.
Results may differ from a plain program's by a relative error of at most 0.00022.
Values sent between devices are 32-bit elements; how exact they have to be, the bound alone decides.
No kernel may reach another device: no remote copies, remote signals or barrier semaphores. Data moves between devices by JAX's collectives and lax.ppermute only.
A program may use at most 256 MiB of HBM per device.

v0:
```python
import jax
import jax.numpy as jnp
from jax import lax
from jax.sharding import PartitionSpec as P


def extended(cells, sides, width, closed):
    for axis, dim in sides:
        count = lax.axis_size(axis)
        ends = count if closed else count - 1
        head = lax.slice_in_dim(cells, 0, width, axis=dim)
        tail = lax.slice_in_dim(cells, cells.shape[dim] - width, cells.shape[dim], axis=dim)
        cells = jnp.concatenate(
            [
                lax.ppermute(tail, axis, [(i, (i + 1) % count) for i in range(ends)]),
                cells,
                lax.ppermute(head, axis, [((i + 1) % count, i) for i in range(ends)]),
            ],
            axis=dim,
        )
    return cells


def centred(padded, axis, count):

    def piece(lower):
        return lax.slice_in_dim(padded, lower, lower + count, axis=axis)

    return (8.0 * (piece(3) - piece(1)) - (piece(4) - piece(0))) / 12.0


def cross(left, right):
    return lax.dot_general(
        left,
        right,
        (((1,), (1,)), ((), ())),
        precision=lax.Precision.HIGHEST,
        preferred_element_type=jnp.float32,
    )


def summed_parts(parts):
    shares = (lax.psum_scatter(parts[0], "lon", scatter_dimension=0, tiled=True),)
    shares = lax.psum((shares[0],), "lat")
    return (lax.all_gather(shares[0], "lon", axis=0, tiled=True),)


def on_device(u_wind, v_wind):
    snaps, lat_rows, lon_cols = u_wind.shape
    n_lat = lat_rows * lax.axis_size("lat")
    n_lon = lon_cols * lax.axis_size("lon")
    ratio = n_lon / (2.0 * n_lat)
    winds = jnp.stack([u_wind, v_wind])
    lon_padded = extended(winds, (("lon", 3),), 2, True)
    lat_padded = extended(winds, (("lat", 2),), 2, False)
    global_rows = (lax.axis_index("lat") * lat_rows + jnp.arange(-2, lat_rows + 2)).astype(
        jnp.float32
    )
    phi = -jnp.pi / 2 + (global_rows + 0.5) * jnp.pi / n_lat
    cosine = jnp.cos(phi)
    root = jnp.sqrt(cosine[2:-2])[:, None]
    along_lon = centred(lon_padded, 3, lon_cols)
    along_lat = centred(lat_padded * cosine[None, None, :, None], 2, lat_rows)
    zeta = (ratio * along_lon[1] - along_lat[0]) / root
    delta = (ratio * along_lon[0] + along_lat[1]) / root
    matrix = jnp.stack([zeta, delta], axis=1).reshape(snaps, -1)
    total = 2.0 * n_lat * n_lon
    gram = summed_parts((cross(matrix, matrix),))[0]
    gram = gram / total
    lower = jnp.linalg.cholesky(gram)
    inverse = jax.scipy.linalg.solve_triangular(
        lower, jnp.eye(snaps, dtype=jnp.float32), lower=True
    )
    basis = jnp.dot(
        inverse, matrix, precision=lax.Precision.HIGHEST, preferred_element_type=jnp.float32
    )
    return (basis.reshape(snaps, 2, lat_rows, lon_cols), lower.T)


def solution(mesh):
    in_specs = (P(None, "lat", "lon"), P(None, "lat", "lon"))
    out_specs = (P(None, None, "lat", "lon"), P())
    return jax.shard_map(
        on_device, mesh=mesh, in_specs=in_specs, out_specs=out_specs, check_vma=False
    )
```

profile of v0, /device:TPU:0, one launch (start us, length us, event | category | flops | bytes accessed | tf_op | source)
XLA Modules:
  0.0 353.3 jit_solution(14856567004534644817)
XLA Ops:
  7.2 10.9 %copy_bitcast_fusion = (f32[1,256,48,128]{3,1,2,0:T(8,128)S(1)}, f32[1,256,48,128]{3,1,2,0:T(8,128)}) fusion(f32[256,48,128]{2,1,0:T(8,128)} %param.3, f32[256,48,128]{2,1,0:T(8,128)} %param.2), kind=kLoop, calls=%fused_computation.34 | loop fusion | bytes 25165824 | tf_op jit(solution)/shard_map/stack | solution.py:53
  18.1 16.8 %fusion = (f32[2,256,48,2]{3,1,2,0:T(8,128)}, f32[2,256,48,2]{3,1,2,0:T(8,128)}) fusion(f32[1,256,48,128]{3,1,2,0:T(8,128)} %get-tuple-element.43, f32[1,256,48,128]{3,1,2,0:T(8,128)S(1)} %get-tuple-element.42), kind=kLoop, calls=%fused_computation.11 | loop fusion | flops 98304 | bytes 12976128 | tf_op jit(solution)/shard_map/stack | solution.py:53
  35.0 7.6 %copy.19 = f32[2,256,48,2]{1,2,3,0:T(8,128)S(1)} copy(f32[2,256,48,2]{3,1,2,0:T(8,128)} %get-tuple-element.30) | data formatting | bytes 393216 | tf_op jit(solution)/shard_map/slice | solution.py:11
  42.6 3.4 collective-permute-start
  46.0 7.6 %copy.21 = f32[2,256,48,2]{1,2,3,0:T(8,128)S(1)} copy(f32[2,256,48,2]{3,1,2,0:T(8,128)} %get-tuple-element.31) | data formatting | bytes 393216 | tf_op jit(solution)/shard_map/slice | solution.py:12
  53.6 1.3 fusion.14
  54.9 3.5 collective-permute-start.2
  58.4 1.5 collective-permute-start.3
  60.0 0.1 slice_sqrt_fusion
  60.1 6.6 %copy.20 = f32[2,256,48,2]{3,1,2,0:T(8,128)} copy(f32[2,256,48,2]{1,2,3,0:T(8,128)S(1)} %collective-permute-done) | data formatting | bytes 393216 | tf_op jit(solution)/shard_map/ppermute | solution.py:17
  66.7 6.6 %copy.22 = f32[2,256,48,2]{3,1,2,0:T(8,128)} copy(f32[2,256,48,2]{1,2,3,0:T(8,128)S(1)} %collective-permute-done.1) | data formatting | bytes 393216 | tf_op jit(solution)/shard_map/ppermute | solution.py:15
  73.2 33.8 %pad_maximum_fusion = (f32[2,256,48,130]{3,1,2,0:T(8,128)}, f32[2,256,48,130]{3,1,2,0:T(8,128)}) fusion(f32[2,256,48,2]{3,1,2,0:T(8,128)} %copy.20, f32[1,256,48,128]{3,1,2,0:T(8,128)} %copy-done, f32[1,256,48,128]{3,1,2,0:T(8,128)} %get-tuple-element.43, f32[2,256,48,2]{3,1,2,0:T(8,128)} %copy.22), kind=kLoop, calls=%fused_computation.2 | loop fusion | flops 12779520 | bytes 38535168 | tf_op jit(solution)/shard_map/concatenate | solution.py:13
  107.1 36.6 %fusion.6 = f32[2,256,48,128]{3,1,2,0:T(8,128)} fusion(f32[2,256,48,130]{3,1,2,0:T(8,128)} %get-tuple-element.29, f32[2,256,48,130]{3,1,2,0:T(8,128)} %get-tuple-element.28), kind=kLoop, calls=%fused_computation.20 | loop fusion | flops 15728640 | bytes 62914560 | tf_op jit(solution)/shard_map/div | solution.py:29
  143.6 5.7 %maximum_multiply_fusion = f32[2,256,52,128]{3,1,2,0:T(8,128)S(1)} fusion(f32[2,256,2,128]{3,1,2,0:T(8,128)} %collective-permute-done.3, f32[1,256,48,128]{3,1,2,0:T(8,128)} %copy-done, f32[1,256,48,128]{3,1,2,0:T(8,128)} %get-tuple-element.43, f32[2,256,2,128]{3,1,2,0:T(8,128)S(1)} %collective-permute-done.2, f32[52]{0:T(128)S(1)} %add_cosine_fusion), kind=kLoop, calls=%fused_computation.10 | loop fusion | flops 13631488 | bytes 27263184 | tf_op jit(solution)/shard_map/mul | solution.py:63
  149.4 7.5 %fusion.3 = f32[2,256,48,128]{3,1,2,0:T(8,128)} fusion(f32[2,256,52,128]{3,1,2,0:T(8,128)S(1)} %maximum_multiply_fusion), kind=kLoop, calls=%fused_computation.15 | loop fusion | flops 15728640 | bytes 62914560 | tf_op jit(solution)/shard_map/div | solution.py:29
  156.8 9.7 %fusion.13 = (f32[256,1,48,128]{3,0,2,1:T(8,128)S(1)}, f32[256,1,48,128]{3,0,2,1:T(8,128)S(1)}) fusion(f32[2,256,48,128]{3,1,2,0:T(8,128)} %fusion.3, f32[2,256,48,128]{3,1,2,0:T(8,128)} %fusion.6, f32[48]{0:T(128)S(1)} %slice_sqrt_fusion), kind=kLoop, calls=%fused_computation.32 | loop fusion | flops 9437184 | bytes 37748928 | tf_op jit(solution)/shard_map/div | solution.py:64
  166.5 2.6 copy-done.1
  169.2 1.9 copy-done.2
  171.0 12.4 %convolution_bitcast_fusion = f32[256,256]{1,0:T(8,128)} fusion(f32[256,1,48,128]{3,0,2,1:T(8,128)S(1)} %get-tuple-element.27, f32[256,1,48,128]{3,0,2,1:T(8,128)S(1)} %get-tuple-element.26), kind=kOutput, calls=%fused_computation.36 | convolution fusion | flops 9666822144 | bytes 12845056 | tf_op jit(solution)/shard_map/dot_general | solution.py:33
  183.5 10.9 %pad_maximum_fusion.1 = f32[256,2,48,128]{3,0,2,1:T(8,128)} fusion(f32[256,1,48,128]{3,0,2,1:T(8,128)} %copy-done.2, f32[256,1,48,128]{3,0,2,1:T(8,128)} %copy-done.1), kind=kLoop, calls=%fused_computation.23 | loop fusion | flops 3145728 | bytes 25165824 | tf_op jit(solution)/shard_map/stack | solution.py:66
  194.4 12.6 %copy.27 = f32[256,2,48,128]{0,3,2,1:T(8,128)} copy(f32[256,2,48,128]{3,0,2,1:T(8,128)} %pad_maximum_fusion.1) | data formatting | bytes 25165824 | tf_op jit(solution)/shard_map/stack | solution.py:66
  207.0 13.1 %reduce-scatter.4.cloned.1.call-done = f32[32,256]{1,0:T(8,128)} async-done(((f32[256,256]{1,0:T(8,128)}), f32[32,256]{1,0:T(8,128)}) %reduce-scatter.4.cloned.1.call-update) | async-done | bytes 32784
  220.1 0.9 copy.34
  220.9 21.1 %psum.7 = f32[32,256]{0,1:T(8,128)S(1)} all-reduce(f32[32,256]{0,1:T(8,128)S(1)} %copy.34), channel_id=1, replica_groups=mesh['lon'=8,'lat'=4] {'lat'}, use_global_device_ids=true, to_apply=%region_1.0 | all-reduce | flops 8192 | bytes 65536 | tf_op jit(solution)/shard_map/psum | solution.py:44
  242.0 0.1 copy.24
  242.1 9.6 %all_gather.3 = f32[256,256]{1,0:T(8,128)S(1)} all-gather(f32[32,256]{1,0:T(8,128)S(1)} %copy.24), channel_id=1, replica_groups=mesh['lon'=8,'lat'=4] {'lon'}, dimensions={0}, use_global_device_ids=true | all-gather | bytes 294912 | tf_op jit(solution)/shard_map/all_gather | solution.py:45
  251.7 0.1 copy.25
  251.9 0.1 copy.26
  252.1 11.7 %cholesky.50 = f32[128,128]{1,0:T(8,128)S(1)} custom-call(f32[128,128]{1,0:T(8,128)S(1)} %cholesky.118), custom_call_target="Cholesky" | custom-call | tf_op jit(solution)/shard_map/jit(cholesky)/cholesky | solution.py:70
  263.8 9.8 %custom-call.15 = f32[1,128,128]{1,2,0:T(8,128)S(1)} custom-call(f32[1,128,128]{2,1,0:T(8,128)S(1)} %get-tuple-element.39), custom_call_target="InvertDiagBlocksLowerTriangular" | custom-call | tf_op jit(solution)/shard_map/jit(cholesky)/cholesky | solution.py:70
  273.7 0.2 constant_dynamic-update-slice_fusion.1
  273.9 0.3 convolution_subtract_fusion.1
  274.1 11.7 %cholesky.105 = f32[128,128]{1,0:T(8,128)S(1)} custom-call(f32[128,128]{1,0:T(8,128)S(1)} %convolution_subtract_fusion.1), custom_call_target="Cholesky" | custom-call | tf_op jit(solution)/shard_map/jit(cholesky)/cholesky | solution.py:70
  285.9 0.6 compare_reduce_fusion
  286.5 0.6 compare_reduce_fusion.1
  288.5 0.1 triangular_solve.63
  288.6 4.4 %while.1 = (s32[]{:T(128)}, f32[256,256]{1,0:T(8,128)S(1)}, s32[2,2]{1,0:T(2,128)S(1)}, f32[2,128,128]{2,1,0:T(8,128)S(1)}, s32[]{:T(128)}) while((s32[]{:T(128)}, f32[256,256]{1,0:T(8,128)S(1)}, s32[2,2]{1,0:T(2,128)S(1)}, f32[2,128,128]{2,1,0:T(8,128)S(1)}, s32[]{:T(128)}) %tuple.35), condition=%wide.while_cond, body=%wide.while_body.sunk | while | flops 2 | bytes 131181 | solution.py:71
  289.0 0.6 fusion.34
  289.6 1.4 bitcast_dynamic-update-slice_fusion.2
  291.0 0.6 fusion.34
  291.6 1.4 bitcast_dynamic-update-slice_fusion.2
  293.0 19.7 %custom-call.16 = f32[2,128,128]{1,2,0:T(8,128)S(1)} custom-call(f32[2,128,128]{2,1,0:T(8,128)S(1)} %get-tuple-element.9), custom_call_target="InvertDiagBlocksLowerTriangular" | custom-call | tf_op jit(solution)/shard_map/jit(_solve_triangular)/triangular_solve | solution.py:71
  312.6 0.3 fusion.20
  312.9 0.3 convolution_subtract_fusion
  313.2 0.3 fusion.23
  313.5 15.3 %fusion.8 = f32[256,2,48,128]{3,0,2,1:T(8,128)} fusion(f32[256,2,48,128]{0,3,2,1:T(8,128)} %copy.27, f32[128,256]{1,0:T(8,128)S(1)} %fusion.23, f32[128,256]{1,0:T(8,128)S(1)} %fusion.20), kind=kOutput, calls=%fused_computation.24 | convolution fusion | flops 9663741952 | bytes 25427968 | tf_op jit(solution)/shard_map/dot_general | solution.py:74
  328.8 16.6 %copy.28 = f32[256,2,48,128]{3,2,1,0:T(8,128)} copy(f32[256,2,48,128]{3,0,2,1:T(8,128)} %fusion.8) | data formatting | bytes 25165824
  345.4 0.8 copy.29
  (24 shorter events, 0.4 us)
Async XLA Ops:
  7.2 212.9 %reduce-scatter.4.cloned.1.call-start = ((), (), s32[]{:S(2)}) async-start(), calls=%async_computation.1 | async-start | bytes 294912
  18.1 16.8 %copy-start = (f32[1,256,48,128]{3,1,2,0:T(8,128)}, f32[1,256,48,128]{3,1,2,0:T(8,128)S(1)}, u32[]{:S(2)}) copy-start(f32[1,256,48,128]{3,1,2,0:T(8,128)S(1)} %get-tuple-element.42) | copy-start | bytes 18874372
  42.6 17.5 %collective-permute-start = (f32[2,256,48,2]{1,2,3,0:T(8,128)S(1)}, f32[2,256,48,2]{1,2,3,0:T(8,128)S(1)}, u32[]{:S(2)}, u32[]{:S(2)}) collective-permute-start(f32[2,256,48,2]{1,2,3,0:T(8,128)S(1)} %copy.19), channel_id=1, source_target_pairs={{4,0},{8,4},{12,8},{16,12},{20,16},{24,20},{28,24},{0,28},{5,1},{9... | collective-permute-start | bytes 589832 | tf_op jit(solution)/shard_map/ppermute | solution.py:17
  53.5 13.1 %collective-permute-start.1 = (f32[2,256,48,2]{1,2,3,0:T(8,128)S(1)}, f32[2,256,48,2]{1,2,3,0:T(8,128)S(1)}, u32[]{:S(2)}, u32[]{:S(2)}) collective-permute-start(f32[2,256,48,2]{1,2,3,0:T(8,128)S(1)} %copy.21), channel_id=1, source_target_pairs={{0,4},{4,8},{8,12},{12,16},{16,20},{20,24},{24,28},{28,0},{1,5},{5... | collective-permute-start | bytes 589832 | tf_op jit(solution)/shard_map/ppermute | solution.py:15
  54.9 88.8 %collective-permute-start.2 = (f32[2,256,2,128]{3,1,2,0:T(8,128)S(1)}, f32[2,256,2,128]{3,1,2,0:T(8,128)S(1)}, u32[]{:S(2)}, u32[]{:S(2)}) collective-permute-start(f32[2,256,2,128]{3,1,2,0:T(8,128)S(1)} %get-tuple-element.32), channel_id=1, source_target_pairs={{0,1},{1,2},{2,3},{4,5},{5,6},{6,7},{8,9},{9,10},{10,11},{12,13},{... | collective-permute-start | bytes 1572872 | tf_op jit(solution)/shard_map/ppermute | solution.py:15
  58.4 85.2 %collective-permute-start.3 = (f32[2,256,2,128]{3,1,2,0:T(8,128)S(1)}, f32[2,256,2,128]{3,1,2,0:T(8,128)}, u32[]{:S(2)}, u32[]{:S(2)}) collective-permute-start(f32[2,256,2,128]{3,1,2,0:T(8,128)S(1)} %get-tuple-element.33), channel_id=1, source_target_pairs={{1,0},{2,1},{3,2},{5,4},{6,5},{7,6},{9,8},{10,9},{11,10},{13,12},{... | collective-permute-start | bytes 1572872 | tf_op jit(solution)/shard_map/ppermute | solution.py:17
  166.5 2.7 copy-start.1
  166.5 4.5 %copy-start.2 = (f32[256,1,48,128]{3,0,2,1:T(8,128)}, f32[256,1,48,128]{3,0,2,1:T(8,128)S(1)}, u32[]{:S(2)}) copy-start(f32[256,1,48,128]{3,0,2,1:T(8,128)S(1)} %get-tuple-element.27) | copy-start | bytes 18874372
Sparse Core Ops, SparseCore 0:
  183.6 36.4 reduce-scatter.3
where the time goes:
time: 359 us; the launch traced here: 353 us
  other arithmetic  177 us (49%)
  local copies, waits for them, and re-layouts  79.1 us (22%)
  blocking collectives  30.7 us (9%)
  matrix products  29 us (8%)
  between operations  15.8 us (4%)
  waiting for transfers between devices  13.1 us (4%)
  starting transfers between devices  8.48 us (2%)
    div x2, other arithmetic, centred(): return (8.0 * (piece(3) - piece(1)) - (piece(4) - piece(0))) / 12.0  44.1 us
    another operation x7, other arithmetic, on_device(): lower = jnp.linalg.cholesky(gram)  34.6 us
    concatenate x1, other arithmetic, extended(): jnp.concatenate([lax.ppermute(tail, axis, [(i, (i + 1) % count) for i in...  33.8 us
    unnamed x9, local copies, waits for them, and re-layouts  22.8 us
    psum x1, blocking collectives, summed_parts(): shares = lax.psum((shares[0],), 'lat')  21.1 us
    another operation x2, other arithmetic, on_device(): jax.scipy.linalg.solve_triangular(lower, jnp.eye(snaps, dtype=jnp.float32...  19.7 us
    another operation x2, other arithmetic, on_device(): winds = jnp.stack([u_wind, v_wind])  18.1 us
    dot_general x1, matrix products, on_device(): jnp.dot(inverse, matrix, precision=lax.Precision.HIGHEST, preferred_eleme...  15.3 us
  transfers between devices with their start and end apart: 5, of which 1 were waited for; matrix products, arithmetic and copies ran while one was open for 33% of the time, Pallas kernels for 0%

commit v1 on v0

v1 whole, which is shorter than its diff:
```python
import functools

import jax
import jax.numpy as jnp
from jax import lax
from jax.experimental import pallas as pl
from jax.experimental.pallas import tpu as pltpu
from jax.sharding import PartitionSpec as P

F32 = jnp.float32
BF16 = jnp.bfloat16
VMEM = pltpu.MemorySpace.VMEM
LANES = 128
HALF = 128
PIECE = HALF + 8
GROUP = 4


def vmem_spec():
    return pl.BlockSpec(memory_space=VMEM)


def smem_spec():
    return pl.BlockSpec(memory_space=pltpu.MemorySpace.SMEM)


def any_spec():
    return pl.BlockSpec(memory_space=pl.ANY)


def in_vmem(x):
    return pltpu.with_memory_space_constraint(x, VMEM)


def in_hbm(x):
    return pltpu.with_memory_space_constraint(x, pltpu.MemorySpace.HBM)


def cost(flops, nbytes):
    return pl.CostEstimate(flops=flops, bytes_accessed=nbytes, transcendentals=0)


def load_body(rows, u_ref, v_ref, ut_ref, vt_ref, west_ref, east_ref, sems):
    snaps = u_ref.shape[0]

    def copy(wind, j):
        src = (u_ref, v_ref)[wind]
        dst = (ut_ref, vt_ref)[wind]
        return pltpu.make_async_copy(src.at[:, j, :], dst.at[j], sems.at[wind, j])

    def start(j, carry):
        copy(0, j).start()
        copy(1, j).start()
        return carry

    lax.fori_loop(0, rows, start, 0)
    step = 64
    lane = lax.broadcasted_iota(jnp.int32, (step, LANES), 1)
    for wind in range(2):
        west_ref[wind] = jnp.zeros((snaps, LANES), F32)
        east_ref[wind] = jnp.zeros((snaps, LANES), F32)

    def pack(j, carry):
        mine = (lane // 2) == j
        for wind in range(2):
            copy(wind, j).wait()
            src = (ut_ref, vt_ref)[wind]
            for t in range(0, snaps, step):
                cells = src[j, t : t + step, :]
                west = pltpu.roll(cells, 2 * j, 1)
                east = pltpu.roll(cells, 2 * j + 2, 1)
                part = pl.ds(t, step)
                west_ref[wind, part, :] = jnp.where(mine, west, west_ref[wind, part, :])
                east_ref[wind, part, :] = jnp.where(mine, east, east_ref[wind, part, :])
        return carry

    lax.fori_loop(0, rows, pack, 0)


def load_and_pack(u, v):
    snaps, rows, cols = u.shape
    turned = VMEM((rows, snaps, cols), F32)
    packed = VMEM((2, snaps, LANES), F32)
    return pl.pallas_call(
        functools.partial(load_body, rows),
        out_shape=(turned, turned, packed, packed),
        in_specs=[any_spec(), any_spec()],
        out_specs=(vmem_spec(),) * 4,
        scratch_shapes=[pltpu.SemaphoreType.DMA((2, rows))],
        compiler_params=pltpu.CompilerParams(vmem_limit_bytes=8 << 20),
        cost_estimate=cost(u.size * 8, u.size * 8),
        name="load_and_pack",
    )(in_hbm(u), in_hbm(v))


def stencil_body(rows, ut_ref, vt_ref, north_ref, south_ref, coef_ref, x_ref):
    snaps = ut_ref.shape[1]
    step = 32

    def one_row(j, u_row, v_row, u_near, v_near):
        lon8, lon1 = coef_ref[j, 0], coef_ref[j, 1]
        lat = [coef_ref[j, 2 + k] for k in range(4)]
        for t in range(0, snaps, step):
            part = pl.ds(t, step)
            for out, (own, near, sign) in enumerate(
                ((v_row, u_near, -1.0), (u_row, v_near, 1.0))
            ):
                cells = own(part)
                one = pltpu.roll(cells, LANES - 1, 1) - pltpu.roll(cells, 1, 1)
                two = pltpu.roll(cells, LANES - 2, 1) - pltpu.roll(cells, 2, 1)
                along = lon8 * one - lon1 * two
                cross = (lat[1] * near[2](part) - lat[0] * near[1](part)) - (
                    lat[3] * near[3](part) - lat[2] * near[0](part)
                )
                x_ref[j, part, out * LANES : (out + 1) * LANES] = (
                    along + cross if sign > 0 else along - cross
                )

    def inner(ref, j):
        return lambda part: ref[j, part, :]

    def getter(ref, wind, j):
        if j < 0:
            return inner(north_ref, wind * 2 + j + 2)
        if j >= rows:
            return inner(south_ref, wind * 2 + j - rows)
        return inner(ref, j)

    def edge(j):
        u_near = [getter(ut_ref, 0, j + d) for d in (-2, -1, 1, 2)]
        v_near = [getter(vt_ref, 1, j + d) for d in (-2, -1, 1, 2)]
        one_row(j, inner(ut_ref, j), inner(vt_ref, j), u_near, v_near)

    def middle(j, carry):
        u_near = [inner(ut_ref, j + d) for d in (-2, -1, 1, 2)]
        v_near = [inner(vt_ref, j + d) for d in (-2, -1, 1, 2)]
        one_row(j, inner(ut_ref, j), inner(vt_ref, j), u_near, v_near)
        return carry

    lax.fori_loop(2, rows - 2, middle, 0)
    for j in (0, 1, rows - 2, rows - 1):
        edge(j)


def differences(ut, vt, north, south, coef):
    rows, snaps, cols = ut.shape
    return pl.pallas_call(
        functools.partial(stencil_body, rows),
        out_shape=VMEM((rows, snaps, 2 * cols), F32),
        in_specs=[vmem_spec()] * 4 + [smem_spec()],
        out_specs=vmem_spec(),
        compiler_params=pltpu.CompilerParams(vmem_limit_bytes=8 << 20),
        cost_estimate=cost(ut.size * 26, ut.size * 16),
        name="differences",
    )(in_vmem(ut), in_vmem(vt), in_vmem(north), in_vmem(south), coef)


def gram_body(
    rows, x_ref, west_ref, east_ref, from_west_ref, from_east_ref, scale_ref,
    hi_ref, lo_ref, out_ref, fix_ref, acc_ref,
):
    snaps = x_ref.shape[1]
    step = 64
    lane = lax.broadcasted_iota(jnp.int32, (step, LANES), 1)
    even = lane % 2 == 0
    even_row = (lane // 2) % 2 == 0
    scale = scale_ref[0:1, :]
    for wind in range(2):
        for t in range(0, snaps, step):
            part = pl.ds(t, step)
            left = from_west_ref[wind, part, :] - east_ref[wind, part, :]
            right = from_east_ref[wind, part, :] - west_ref[wind, part, :]
            left = scale * (left - jnp.where(even, 8.0 * pltpu.roll(left, LANES - 1, 1), 0.0))
            right = scale * (jnp.where(even, 0.0, 8.0 * pltpu.roll(right, 1, 1)) - right)
            right = pltpu.roll(right, LANES - 2, 1)
            fix_ref[wind, 0, part, :] = jnp.where(even_row, left, right)
            fix_ref[wind, 1, part, :] = jnp.where(even_row, right, left)
    acc_ref[...] = jnp.zeros_like(acc_ref)
    outer = jnp.logical_or(lane < 2, lane >= LANES - 2)

    def group(i, carry):
        base = i * GROUP
        for k in range(GROUP):
            j = base + k
            shift = lax.rem(2 * LANES - 2 * j, LANES)
            for out in range(2):
                for t in range(0, snaps, step):
                    part = pl.ds(t, step)
                    fix = pltpu.roll(fix_ref[1 - out, k % 2, part, :], shift, 1)
                    span = slice(out * LANES, (out + 1) * LANES)
                    x = x_ref[j, part, span] + jnp.where(outer, fix, 0.0)
                    hi = x.astype(BF16)
                    hi_ref[j, part, span] = hi
                    lo_ref[j, part, span] = (x - hi.astype(F32)).astype(BF16)
        total = None
        for k in range(GROUP):
            hi = hi_ref[base + k]
            both = jnp.concatenate([hi, lo_ref[base + k]], axis=0)
            term = lax.dot_general(
                hi, both, (((1,), (1,)), ((), ())), preferred_element_type=F32
            )
            total = term if total is None else total + term
        acc_ref[...] += total
        return carry

    lax.fori_loop(0, rows // GROUP, group, 0)
    low = acc_ref[:, snaps:]
    gram = acc_ref[:, :snaps] + (low + low.T)
    row = lax.broadcasted_iota(jnp.int32, (HALF, HALF), 0)
    col = lax.broadcasted_iota(jnp.int32, (HALF, HALF), 1)
    first = gram[:HALF, :HALF]
    second = gram[HALF:, HALF:]
    out_ref[0, :HALF, :] = gram[HALF:, :HALF]
    out_ref[1, :HALF, :] = jnp.where(row >= col, first, second)
    diagonal = jnp.sum(jnp.where(row == col, second, 0.0), axis=0, keepdims=True)
    out_ref[0, HALF:, :] = jnp.broadcast_to(diagonal, (8, HALF))
    out_ref[1, HALF:, :] = jnp.zeros((8, HALF), F32)


def partial_gram(x, west, east, from_west, from_east, scale):
    rows, snaps, both = x.shape
    halves = VMEM((rows, snaps, both), BF16)
    return pl.pallas_call(
        functools.partial(gram_body, rows),
        out_shape=(halves, halves, VMEM((2, PIECE, HALF), F32)),
        in_specs=[vmem_spec()] * 6,
        out_specs=(vmem_spec(),) * 3,
        scratch_shapes=[
            pltpu.VMEM((2, 2, snaps, LANES), F32),
            pltpu.VMEM((snaps, 2 * snaps), F32),
        ],
        compiler_params=pltpu.CompilerParams(vmem_limit_bytes=12 << 20),
        cost_estimate=cost(x.size * 1024, x.size * 8),
        name="partial_gram",
    )(in_vmem(x), in_vmem(west), in_vmem(east), in_vmem(from_west), in_vmem(from_east), scale)


def swap(x, axis, bit):
    count = lax.axis_size(axis)
    return lax.ppermute(x, axis, [(i, i ^ bit) for i in range(count)])


def powers(count):
    bit = 1
    while bit < count:
        yield bit
        bit *= 2


def summed(parts):
    odd = lax.axis_index("lon") % 2 == 1
    mine = jnp.where(odd, parts[1], parts[0])
    other = jnp.where(odd, parts[0], parts[1])
    mine = mine + swap(other, "lon", 1)
    for bit in powers(lax.axis_size("lat")):
        mine = mine + swap(mine, "lat", bit)
    for bit in powers(lax.axis_size("lon")):
        if bit > 1:
            mine = mine + swap(mine, "lon", bit)
    theirs = swap(mine, "lon", 1)
    return jnp.where(odd, theirs, mine), jnp.where(odd, mine, theirs)


def dot_nt(a, b):
    return lax.dot_general(
        a, b, (((1,), (1,)), ((), ())), precision=lax.Precision.HIGHEST, preferred_element_type=F32
    )


def dot_nn(a, b):
    return lax.dot_general(
        a, b, (((1,), (0,)), ((), ())), precision=lax.Precision.HIGHEST, preferred_element_type=F32
    )


def eliminate(matrix):
    size = matrix.shape[0]
    groups = size // 8
    row = lax.broadcasted_iota(jnp.int32, (8, size), 0)
    col = lax.broadcasted_iota(jnp.int32, (8, size), 1)
    work = [matrix[8 * g : 8 * g + 8, :] for g in range(groups)]
    right = [jnp.where(col == row + 8 * g, 1.0, 0.0) for g in range(groups)]
    for k in range(size):
        g, r = divmod(k, 8)
        pivot_row = jnp.broadcast_to(work[g][r : r + 1, :], (8, size))
        right_row = jnp.broadcast_to(right[g][r : r + 1, :], (8, size))
        pivot = jnp.broadcast_to(pivot_row[:, k : k + 1], (8, size))
        inverse = 1.0 / pivot
        for h in range(g, groups):
            factor = jnp.broadcast_to(work[h][:, k : k + 1], (8, size)) * inverse
            if h == g:
                factor = jnp.where(row > r, factor, 0.0)
            work[h] = work[h] - factor * pivot_row
            right[h] = right[h] - factor * right_row
    upper, lower = [], []
    for g in range(groups):
        diagonal = jnp.sum(jnp.where(col == row + 8 * g, work[g], 0.0), axis=1, keepdims=True)
        root = lax.rsqrt(diagonal)
        upper.append(jnp.where(col >= row + 8 * g, work[g] * root, 0.0))
        lower.append(right[g] * root)
    return jnp.concatenate(upper, axis=0), jnp.concatenate(lower, axis=0)


def factor_body(total, corner_ref, mixed_ref, r_ref, hi_ref, lo_ref):
    inv = 1.0 / total
    row = lax.broadcasted_iota(jnp.int32, (HALF, HALF), 0)
    col = lax.broadcasted_iota(jnp.int32, (HALF, HALF), 1)
    mixed = mixed_ref[:HALF, :] * inv
    corner = corner_ref[:HALF, :] * inv
    diagonal = corner_ref[HALF : HALF + 1, :] * inv
    turned = mixed.T
    first = jnp.where(row >= col, mixed, turned)
    second = jnp.where(row < col, mixed, jnp.where(row > col, turned, diagonal))
    r11, w11 = eliminate(first)
    l21 = dot_nt(corner, w11)
    r22, w22 = eliminate(second - dot_nt(l21, l21))
    w21 = -dot_nn(w22, dot_nn(l21, w11))
    zero = jnp.zeros((HALF, HALF), F32)
    r_ref[:HALF, :HALF] = r11
    r_ref[:HALF, HALF:] = l21.T
    r_ref[HALF:, :HALF] = zero
    r_ref[HALF:, HALF:] = r22
    for i, j, w in ((0, 0, w11), (0, 1, zero), (1, 0, w21), (1, 1, w22)):
        part = (slice(i * HALF, (i + 1) * HALF), slice(j * HALF, (j + 1) * HALF))
        hi = w.astype(BF16)
        hi_ref[part] = hi
        lo_ref[part] = (w - hi.astype(F32)).astype(BF16)


def factor(corner, mixed, total):
    snaps = 2 * HALF
    return pl.pallas_call(
        functools.partial(factor_body, total),
        out_shape=(
            VMEM((snaps, snaps), F32),
            VMEM((snaps, snaps), BF16),
            VMEM((snaps, snaps), BF16),
        ),
        in_specs=[vmem_spec()] * 2,
        out_specs=(vmem_spec(),) * 3,
        compiler_params=pltpu.CompilerParams(vmem_limit_bytes=12 << 20),
        cost_estimate=cost(1 << 26, 1 << 20),
        name="factor",
    )(in_vmem(corner), in_vmem(mixed))


def basis_body(rows, whi_ref, wlo_ref, hi_ref, lo_ref, out_ref, buf_ref, sems):
    slots = buf_ref.shape[0]
    cols = out_ref.shape[3]

    def copy(j, slot, part):
        return pltpu.make_async_copy(
            buf_ref.at[slot, :, pl.ds(part * cols, cols)],
            out_ref.at[:, part, j, :],
            sems.at[slot, part],
        )

    weights = jnp.concatenate([whi_ref[...], whi_ref[...], wlo_ref[...]], axis=1)

    def step(j, carry):
        slot = lax.rem(j, slots)

        @pl.when(j >= slots)
        def _():
            copy(j - slots, slot, 0).wait()
            copy(j - slots, slot, 1).wait()

        cells = jnp.concatenate([hi_ref[j], lo_ref[j], hi_ref[j]], axis=0)
        buf_ref[slot] = lax.dot_general(
            weights, cells, (((1,), (0,)), ((), ())), preferred_element_type=F32
        )
        copy(j, slot, 0).start()
        copy(j, slot, 1).start()
        return carry

    lax.fori_loop(0, rows, step, 0)

    def drain(j, carry):
        slot = lax.rem(j, slots)
        copy(j, slot, 0).wait()
        copy(j, slot, 1).wait()
        return carry

    lax.fori_loop(rows - slots, rows, drain, 0)


def basis(whi, wlo, hi, lo):
    rows, snaps, both = hi.shape
    cols = both // 2
    slots = 8
    return pl.pallas_call(
        functools.partial(basis_body, rows),
        out_shape=jax.ShapeDtypeStruct((snaps, 2, rows, cols), F32),
        in_specs=[vmem_spec()] * 4,
        out_specs=any_spec(),
        scratch_shapes=[
            pltpu.VMEM((slots, snaps, both), F32),
            pltpu.SemaphoreType.DMA((slots, 2)),
        ],
        compiler_params=pltpu.CompilerParams(vmem_limit_bytes=8 << 20),
        cost_estimate=cost(hi.size * 1536, hi.size * 8),
        name="basis",
    )(in_vmem(whi), in_vmem(wlo), in_vmem(hi), in_vmem(lo))


def rim(u, v, low, high):
    rows = jnp.stack([u[:, low:high, :], v[:, low:high, :]])
    return rows.transpose(0, 2, 1, 3).reshape(2 * (high - low), u.shape[0], u.shape[2])


def on_device(u, v):
    snaps, rows, cols = u.shape
    n_lat = rows * lax.axis_size("lat")
    lat, lon = lax.axis_size("lat"), lax.axis_size("lon")
    n_lon = cols * lon
    ratio = n_lon / (2.0 * n_lat)

    north = lax.ppermute(rim(u, v, rows - 2, rows), "lat", [(i, i + 1) for i in range(lat - 1)])
    south = lax.ppermute(rim(u, v, 0, 2), "lat", [(i + 1, i) for i in range(lat - 1)])

    index = (lax.axis_index("lat") * rows + jnp.arange(-2, rows + 2)).astype(F32)
    cosine = jnp.cos(-jnp.pi / 2 + (index + 0.5) * jnp.pi / n_lat)
    root = 1.0 / (12.0 * jnp.sqrt(cosine[2:-2]))
    along = ratio * root
    coef = jnp.stack(
        [
            8.0 * along,
            along,
            8.0 * cosine[1:-3] * root,
            8.0 * cosine[3:-1] * root,
            cosine[:-4] * root,
            cosine[4:] * root,
        ],
        axis=1,
    )
    scale = jnp.broadcast_to(
        jnp.pad(jnp.repeat(along, 2), (0, LANES - 2 * rows))[None, :], (8, LANES)
    )

    ut, vt, west, east = load_and_pack(u, v)
    from_west = lax.ppermute(east, "lon", [(i, (i + 1) % lon) for i in range(lon)])
    from_east = lax.ppermute(west, "lon", [((i + 1) % lon, i) for i in range(lon)])
    x = differences(ut, vt, north, south, coef)
    hi, lo, parts = partial_gram(x, west, east, from_west, from_east, scale)
    corner, mixed = summed(parts)
    r, whi, wlo = factor(corner, mixed, 2.0 * n_lat * n_lon)
    return basis(whi, wlo, hi, lo), r


def solution(mesh):
    in_specs = (P(None, "lat", "lon"), P(None, "lat", "lon"))
    out_specs = (P(None, None, "lat", "lon"), P())
    return jax.shard_map(
        on_device, mesh=mesh, in_specs=in_specs, out_specs=out_specs, check_vma=False
    )
```

time: 359 us -> 138 us (0.38); the launches traced: 353 us -> 138 us
  other arithmetic: 177 us -> 0.77 us
  Pallas kernels: 0 us -> 90 us
  local copies, waits for them, and re-layouts: 79.1 us -> 15.5 us
  blocking collectives: 30.7 us -> 0 us
  matrix products: 29 us -> 0 us
  between operations: 15.8 us -> 0.81 us
  starting transfers between devices: 8.48 us -> 16.9 us
    pallas_call x0 -> x5, Pallas kernels: none -> 90 us  [the longest x1 34.9 us: factor(): pl.pallas_call(functools.partial(factor_body, total), out_shape=(VMEM((sn...]
    another operation x12 -> x1, other arithmetic: 83.3 us -> 0.08 us  [on_device(): jnp.stack([8.0 * along, along, 8.0 * cosine[1:-3] * root, 8.0 * cosine[3:...]
    div x5 -> x0, other arithmetic: 53.8 us -> none  [the longest x2 44.1 us: centred(): return (8.0 * (piece(3) - piece(1)) - (piece(4) - piece(0))) / 12.0]
    concatenate x1 -> x0, other arithmetic: 33.8 us -> none  [extended(): jnp.concatenate([lax.ppermute(tail, axis, [(i, (i + 1) % count) for i in...]
    dot_general x2 -> x0, matrix products: 27.7 us -> none  [the longest x1 15.3 us: on_device(): jnp.dot(inverse, matrix, precision=lax.Precision.HIGHEST, preferred_eleme...]
    another operation x11 -> x4, local copies, waits for them, and re-layouts: 27.6 us -> 3.61 us  [the longest x2 3.48 us: rim(): rows = jnp.stack([u[:, low:high, :], v[:, low:high, :]])]
    psum x1 -> x0, blocking collectives: 21.1 us -> none  [summed_parts(): shares = lax.psum((shares[0],), 'lat')]
    slice x2 -> x0, local copies, waits for them, and re-layouts: 15.2 us -> none  [the longest x1 7.58 us: extended(): head = lax.slice_in_dim(cells, 0, width, axis=dim)]
  transfers between devices with their start and end apart: 5 -> 10, of which waited for: 1 -> 6; matrix products, arithmetic and copies ran while one was open for 33% -> 0% of each run, Pallas kernels for 0% -> 23%
where the time goes in v1:
time: 138 us
  Pallas kernels  90 us (65%)
  starting transfers between devices  16.9 us (12%)
  local copies, waits for them, and re-layouts  15.5 us (11%)
  waiting for transfers between devices  14 us (10%)
    pallas_call x1, Pallas kernels, factor(): pl.pallas_call(functools.partial(factor_body, total), out_shape=(VMEM((sn...  34.9 us
    pallas_call x1, Pallas kernels, differences(): pl.pallas_call(functools.partial(stencil_body, rows), out_shape=VMEM((row...  17.1 us
    pallas_call x1, Pallas kernels, load_and_pack(): pl.pallas_call(functools.partial(load_body, rows), out_shape=(turned, tur...  15 us
    pallas_call x1, Pallas kernels, basis(): pl.pallas_call(functools.partial(basis_body, rows), out_shape=jax.ShapeDt...  14.2 us
    ppermute x6, waiting for transfers between devices, swap(): return lax.ppermute(x, axis, [(i, i ^ bit) for i in range(count)])  14 us
    unnamed x9, local copies, waits for them, and re-layouts  11.6 us
    pallas_call x1, Pallas kernels, partial_gram(): pl.pallas_call(functools.partial(gram_body, rows), out_shape=(halves, hal...  8.79 us
    ppermute x6, starting transfers between devices, swap(): return lax.ppermute(x, axis, [(i, i ^ bit) for i in range(count)])  7.94 us
  transfers between devices with their start and end apart: 10, of which 6 were waited for; matrix products, arithmetic and copies ran while one was open for 0% of the time, Pallas kernels for 23%

profile of v1, /device:TPU:0, one launch (start us, length us, event | category | flops | bytes accessed | tf_op | source)
XLA Modules:
  0.0 137.9 jit_solution(2009984784750177486)
XLA Ops:
  0.6 1.7 %slice_bitcast_fusion.1 = (f32[1,256,2,128]{3,2,1,0:T(2,128)S(1)}, f32[1,256,2,128]{3,2,1,0:T(2,128)S(1)}) fusion(f32[256,48,128]{2,1,0:T(8,128)} %u_ref.1), kind=kLoop, calls=%fused_computation.3 | loop fusion | bytes 1048576 | tf_op jit(solution)/shard_map/stack | solution.py:407
  2.4 1.7 %slice_bitcast_fusion = (f32[1,256,2,128]{3,2,1,0:T(2,128)S(1)}, f32[1,256,2,128]{3,2,1,0:T(2,128)S(1)}) fusion(f32[256,48,128]{2,1,0:T(8,128)} %v_ref.1), kind=kLoop, calls=%fused_computation.2 | loop fusion | bytes 1048576 | tf_op jit(solution)/shard_map/stack | solution.py:407
  4.1 0.5 maximum_bitcast_fusion
  4.6 5.0 %collective-permute-start = (f32[4,256,128]{2,1,0:T(8,128)S(1)}, f32[4,256,128]{2,1,0:T(8,128)S(1)}, u32[]{:S(2)}, u32[]{:S(2)}) collective-permute-start(f32[4,256,128]{2,1,0:T(8,128)S(1)} %bitcast.30), channel_id=1, source_target_pairs={{0,1},{1,2},{2,3},{4,5},{5,6},{6,7},{8,9},{9,10},{10,11},{12,13},{... | collective-permute-start | bytes 1572872 | tf_op jit(solution)/shard_map/ppermute | solution.py:418
  9.7 1.3 collective-permute-start.1
  11.0 15.0 %load_and_pack.1 = (f32[48,256,128]{2,1,0:T(8,128)S(1)}, f32[48,256,128]{2,1,0:T(8,128)S(1)}, f32[2,256,128]{2,1,0:T(8,128)S(1)}, f32[2,256,128]{2,1,0:T(8,128)S(1)}) custom-call(f32[256,48,128]{2,1,0:T(8,128)} %u_ref.1, f32[256,48,128]{2,1,0:T(8,128)} %v_ref.1), custom_call_target="tpu_custom_call" | custom-call | flops 12582912 | bytes 12582912 | tf_op jit(solution)/shard_map/load_and_pack/pallas_call | solution.py:84
  25.9 0.0 copy-start
  26.0 2.7 %copy-done = f32[48,256,128]{2,1,0:T(8,128)} copy-done((f32[48,256,128]{2,1,0:T(8,128)}, f32[48,256,128]{2,1,0:T(8,128)S(1)}, u32[]{:S(2)}) %copy-start) | copy-done | bytes 6291480
  28.6 0.0 copy-start.2
  28.7 2.7 %copy-done.2 = f32[48,256,128]{2,1,0:T(8,128)} copy-done((f32[48,256,128]{2,1,0:T(8,128)}, f32[48,256,128]{2,1,0:T(8,128)S(1)}, u32[]{:S(2)}) %copy-start.2) | copy-done | bytes 6291480
  31.3 0.0 collective-permute-start.2
  31.3 2.6 %collective-permute-start.3 = (f32[2,256,128]{2,1,0:T(8,128)S(1)}, f32[2,256,128]{2,1,0:T(8,128)S(1)}, u32[]{:S(2)}, u32[]{:S(2)}) collective-permute-start(f32[2,256,128]{2,1,0:T(8,128)S(1)} %get-tuple-element.14.west_ref), channel_id=1, source_target_pairs={{4,0},{8,4},{12,8},{16,12},{20,16},{24,20},{28,24},{0,28},{5,1},{9... | collective-permute-start | bytes 786440 | tf_op jit(solution)/shard_map/ppermute | solution.py:442
  34.0 0.1 broadcast_multiply_fusion
  34.1 0.1 multiply_bitcast_fusion
  34.2 0.1 copy.22.coef_ref
  34.3 0.1 broadcast_in_dim.4
  34.4 0.1 reshape.20
  34.5 0.0 collective-permute-done.north_ref
  34.5 0.0 collective-permute-done.1.south_ref
  34.5 0.0 copy-start.1
  34.5 2.8 %copy-done.1 = f32[48,256,128]{2,1,0:T(8,128)S(1)} copy-done((f32[48,256,128]{2,1,0:T(8,128)S(1)}, f32[48,256,128]{2,1,0:T(8,128)}, u32[]{:S(2)}) %copy-start.1) | copy-done | bytes 6291480
  37.3 0.0 copy-start.3
  37.3 2.8 %copy-done.3 = f32[48,256,128]{2,1,0:T(8,128)S(1)} copy-done((f32[48,256,128]{2,1,0:T(8,128)S(1)}, f32[48,256,128]{2,1,0:T(8,128)}, u32[]{:S(2)}) %copy-start.3) | copy-done | bytes 6291480
  40.1 17.1 %differences.1.x_ref = f32[48,256,256]{2,1,0:T(8,128)S(1)} custom-call(f32[48,256,128]{2,1,0:T(8,128)S(1)} %copy-done.1, f32[48,256,128]{2,1,0:T(8,128)S(1)} %copy-done.3, f32[4,256,128]{2,1,0:T(8,128)S(1)} %collective-permute-done.north_ref, f32[4,256,128]{2,1,0:T(8,128)S(1)} %collective-permute-done.1.south_ref, f32[48,6]{1,0:T(8,128)S(1)} %copy.22.coef_ref), custom_call_target="tpu_custom_call" | custom-call | flops 40894464 | bytes 25165824 | tf_op jit(solution)/shard_map/differences/pallas_call | solution.py:147
  57.2 0.0 collective-permute-done.2.from_west_ref
  57.2 0.0 collective-permute-done.3.from_east_ref
  57.2 8.8 %partial_gram.1 = (bf16[48,256,256]{2,1,0:T(8,128)(2,1)S(1)}, bf16[48,256,256]{2,1,0:T(8,128)(2,1)S(1)}, f32[2,136,128]{2,1,0:T(8,128)S(1)}) custom-call(f32[48,256,256]{2,1,0:T(8,128)S(1)} %differences.1.x_ref, f32[2,256,128]{2,1,0:T(8,128)S(1)} %get-tuple-element.14.west_ref, f32[2,256,128]{2,1,0:T(8,128)S(1)} %get-tuple-element.15.east_ref, ...), custom_call_target="tpu_custom_call" | custom-call | flops 3221225472 | bytes 25165824 | tf_op jit(solution)/shard_map/partial_gram/pallas_call | solution.py:223
  66.0 0.1 collective-permute-start.4
  66.1 1.2 collective-permute-done.4
  67.4 2.7 %collective-permute-start.5 = (f32[136,128]{1,0:T(8,128)S(1)}, f32[136,128]{1,0:T(8,128)S(1)}, u32[]{:S(2)}, u32[]{:S(2)}) collective-permute-start(f32[136,128]{1,0:T(8,128)S(1)} %bitcast_add_fusion), channel_id=1, source_target_pairs={{0,1},{1,0},{2,3},{3,2},{4,5},{5,4},{6,7},{7,6},{8,9},{9,8},{10,11... | collective-permute-start | bytes 208904 | tf_op jit(solution)/shard_map/ppermute | solution.py:240
  70.1 2.5 %collective-permute-done.5 = f32[136,128]{1,0:T(8,128)S(1)} collective-permute-done((f32[136,128]{1,0:T(8,128)S(1)}, f32[136,128]{1,0:T(8,128)S(1)}, u32[]{:S(2)}, u32[]{:S(2)}) %collective-permute-start.5) | collective-permute-done | bytes 69664 | tf_op jit(solution)/shard_map/ppermute | solution.py:240
  72.6 2.9 %collective-permute-start.6 = (f32[136,128]{1,0:T(8,128)S(1)}, f32[136,128]{1,0:T(8,128)S(1)}, u32[]{:S(2)}, u32[]{:S(2)}) collective-permute-start(f32[136,128]{1,0:T(8,128)S(1)} %add.55), channel_id=1, source_target_pairs={{0,2},{1,3},{2,0},{3,1},{4,6},{5,7},{6,4},{7,5},{8,10},{9,11},{10,... | collective-permute-start | bytes 208904 | tf_op jit(solution)/shard_map/ppermute | solution.py:240
  75.4 2.5 %collective-permute-done.6 = f32[136,128]{1,0:T(8,128)S(1)} collective-permute-done((f32[136,128]{1,0:T(8,128)S(1)}, f32[136,128]{1,0:T(8,128)S(1)}, u32[]{:S(2)}, u32[]{:S(2)}) %collective-permute-start.6) | collective-permute-done | bytes 69664 | tf_op jit(solution)/shard_map/ppermute | solution.py:240
  78.0 0.7 collective-permute-start.7
  78.6 3.7 %collective-permute-done.7 = f32[136,128]{1,0:T(8,128)S(1)} collective-permute-done((f32[136,128]{1,0:T(8,128)S(1)}, f32[136,128]{1,0:T(8,128)S(1)}, u32[]{:S(2)}, u32[]{:S(2)}) %collective-permute-start.7) | collective-permute-done | bytes 69664 | tf_op jit(solution)/shard_map/ppermute | solution.py:240
  82.3 1.6 %collective-permute-start.8 = (f32[136,128]{1,0:T(8,128)S(1)}, f32[136,128]{1,0:T(8,128)S(1)}, u32[]{:S(2)}, u32[]{:S(2)}) collective-permute-start(f32[136,128]{1,0:T(8,128)S(1)} %add.57), channel_id=1, source_target_pairs={{0,16},{4,20},{8,24},{12,28},{16,0},{20,4},{24,8},{28,12},{1,17},{... | collective-permute-start | bytes 208904 | tf_op jit(solution)/shard_map/ppermute | solution.py:240
  83.9 2.8 %collective-permute-done.8 = f32[136,128]{1,0:T(8,128)S(1)} collective-permute-done((f32[136,128]{1,0:T(8,128)S(1)}, f32[136,128]{1,0:T(8,128)S(1)}, u32[]{:S(2)}, u32[]{:S(2)}) %collective-permute-start.8) | collective-permute-done | bytes 69664 | tf_op jit(solution)/shard_map/ppermute | solution.py:240
  86.7 0.1 collective-permute-start.9
  86.8 1.2 collective-permute-done.9
  88.1 34.9 %factor.1 = (f32[256,256]{1,0:T(8,128)S(1)}, bf16[256,256]{1,0:T(8,128)(2,1)S(1)}, bf16[256,256]{1,0:T(8,128)(2,1)S(1)}) custom-call(f32[136,128]{1,0:T(8,128)S(1)} %get-tuple-element.29.corner_ref, f32[136,128]{1,0:T(8,128)S(1)} %get-tuple-element.28.mixed_ref), custom_call_target="tpu_custom_call" | custom-call | flops 67108864 | bytes 1048576 | tf_op jit(solution)/shard_map/factor/pallas_call | solution.py:332
  123.0 0.7 copy.23
  123.7 14.2 %basis.1 = f32[256,2,48,128]{3,2,1,0:T(8,128)} custom-call(bf16[256,256]{1,0:T(8,128)(2,1)S(1)} %get-tuple-element.17.whi_ref, bf16[256,256]{1,0:T(8,128)(2,1)S(1)} %get-tuple-element.18.wlo_ref, bf16[48,256,256]{2,1,0:T(8,128)(2,1)S(1)} %get-tuple-element.19.hi_ref, bf16[48,256,256]{2,1,0:T(8,128)(2,1)S(1)} %get-tuple-element.20.lo_ref), custom_call_target="tpu_custom_call" | custom-call | flops 4831838208 | bytes 25165824 | tf_op jit(solution)/shard_map/basis/pallas_call | solution.py:391
  (13 shorter events, 0.2 us)
Async XLA Ops:
  4.6 29.9 %collective-permute-start = (f32[4,256,128]{2,1,0:T(8,128)S(1)}, f32[4,256,128]{2,1,0:T(8,128)S(1)}, u32[]{:S(2)}, u32[]{:S(2)}) collective-permute-start(f32[4,256,128]{2,1,0:T(8,128)S(1)} %bitcast.30), channel_id=1, source_target_pairs={{0,1},{1,2},{2,3},{4,5},{5,6},{6,7},{8,9},{9,10},{10,11},{12,13},{... | collective-permute-start | bytes 1572872 | tf_op jit(solution)/shard_map/ppermute | solution.py:418
  9.7 24.8 %collective-permute-start.1 = (f32[4,256,128]{2,1,0:T(8,128)S(1)}, f32[4,256,128]{2,1,0:T(8,128)S(1)}, u32[]{:S(2)}, u32[]{:S(2)}) collective-permute-start(f32[4,256,128]{2,1,0:T(8,128)S(1)} %bitcast.31), channel_id=1, source_target_pairs={{1,0},{2,1},{3,2},{5,4},{6,5},{7,6},{9,8},{10,9},{11,10},{13,12},{... | collective-permute-start | bytes 1572872 | tf_op jit(solution)/shard_map/ppermute | solution.py:419
  25.9 2.7 %copy-start = (f32[48,256,128]{2,1,0:T(8,128)}, f32[48,256,128]{2,1,0:T(8,128)S(1)}, u32[]{:S(2)}) copy-start(f32[48,256,128]{2,1,0:T(8,128)S(1)} %get-tuple-element.12.ut_ref) | copy-start | bytes 18874372
  28.6 2.7 %copy-start.2 = (f32[48,256,128]{2,1,0:T(8,128)}, f32[48,256,128]{2,1,0:T(8,128)S(1)}, u32[]{:S(2)}) copy-start(f32[48,256,128]{2,1,0:T(8,128)S(1)} %get-tuple-element.13.vt_ref) | copy-start | bytes 18874372
  31.3 25.9 %collective-permute-start.2 = (f32[2,256,128]{2,1,0:T(8,128)S(1)}, f32[2,256,128]{2,1,0:T(8,128)S(1)}, u32[]{:S(2)}, u32[]{:S(2)}) collective-permute-start(f32[2,256,128]{2,1,0:T(8,128)S(1)} %get-tuple-element.15.east_ref), channel_id=1, source_target_pairs={{0,4},{4,8},{8,12},{12,16},{16,20},{20,24},{24,28},{28,0},{1,5},{5... | collective-permute-start | bytes 786440 | tf_op jit(solution)/shard_map/ppermute | solution.py:441
  31.3 25.9 %collective-permute-start.3 = (f32[2,256,128]{2,1,0:T(8,128)S(1)}, f32[2,256,128]{2,1,0:T(8,128)S(1)}, u32[]{:S(2)}, u32[]{:S(2)}) collective-permute-start(f32[2,256,128]{2,1,0:T(8,128)S(1)} %get-tuple-element.14.west_ref), channel_id=1, source_target_pairs={{4,0},{8,4},{12,8},{16,12},{20,16},{24,20},{28,24},{0,28},{5,1},{9... | collective-permute-start | bytes 786440 | tf_op jit(solution)/shard_map/ppermute | solution.py:442
  34.5 2.8 %copy-start.1 = (f32[48,256,128]{2,1,0:T(8,128)S(1)}, f32[48,256,128]{2,1,0:T(8,128)}, u32[]{:S(2)}) copy-start(f32[48,256,128]{2,1,0:T(8,128)} %copy-done) | copy-start | bytes 18874372
  37.3 2.8 %copy-start.3 = (f32[48,256,128]{2,1,0:T(8,128)S(1)}, f32[48,256,128]{2,1,0:T(8,128)}, u32[]{:S(2)}) copy-start(f32[48,256,128]{2,1,0:T(8,128)} %copy-done.2) | copy-start | bytes 18874372
  66.0 1.3 collective-permute-start.4
  67.4 5.2 %collective-permute-start.5 = (f32[136,128]{1,0:T(8,128)S(1)}, f32[136,128]{1,0:T(8,128)S(1)}, u32[]{:S(2)}, u32[]{:S(2)}) collective-permute-start(f32[136,128]{1,0:T(8,128)S(1)} %bitcast_add_fusion), channel_id=1, source_target_pairs={{0,1},{1,0},{2,3},{3,2},{4,5},{5,4},{6,7},{7,6},{8,9},{9,8},{10,11... | collective-permute-start | bytes 208904 | tf_op jit(solution)/shard_map/ppermute | solution.py:240
  72.6 5.4 %collective-permute-start.6 = (f32[136,128]{1,0:T(8,128)S(1)}, f32[136,128]{1,0:T(8,128)S(1)}, u32[]{:S(2)}, u32[]{:S(2)}) collective-permute-start(f32[136,128]{1,0:T(8,128)S(1)} %add.55), channel_id=1, source_target_pairs={{0,2},{1,3},{2,0},{3,1},{4,6},{5,7},{6,4},{7,5},{8,10},{9,11},{10,... | collective-permute-start | bytes 208904 | tf_op jit(solution)/shard_map/ppermute | solution.py:240
  78.0 4.4 %collective-permute-start.7 = (f32[136,128]{1,0:T(8,128)S(1)}, f32[136,128]{1,0:T(8,128)S(1)}, u32[]{:S(2)}, u32[]{:S(2)}) collective-permute-start(f32[136,128]{1,0:T(8,128)S(1)} %add.56), channel_id=1, source_target_pairs={{0,8},{4,12},{8,0},{12,4},{16,24},{20,28},{24,16},{28,20},{1,9},{5... | collective-permute-start | bytes 208904 | tf_op jit(solution)/shard_map/ppermute | solution.py:240
  82.3 4.4 %collective-permute-start.8 = (f32[136,128]{1,0:T(8,128)S(1)}, f32[136,128]{1,0:T(8,128)S(1)}, u32[]{:S(2)}, u32[]{:S(2)}) collective-permute-start(f32[136,128]{1,0:T(8,128)S(1)} %add.57), channel_id=1, source_target_pairs={{0,16},{4,20},{8,24},{12,28},{16,0},{20,4},{24,8},{28,12},{1,17},{... | collective-permute-start | bytes 208904 | tf_op jit(solution)/shard_map/ppermute | solution.py:240
  86.7 1.3 collective-permute-start.9

commit v2 on v1

v2 whole, which is shorter than its diff:
```python
import functools

import jax
import jax.numpy as jnp
from jax import lax
from jax.experimental import pallas as pl
from jax.experimental.pallas import tpu as pltpu
from jax.sharding import PartitionSpec as P

F32 = jnp.float32
BF16 = jnp.bfloat16
VMEM = pltpu.MemorySpace.VMEM
LANES = 128
HALF = 128
PIECE = HALF + 8
GROUP = 4


def vmem_spec():
    return pl.BlockSpec(memory_space=VMEM)


def smem_spec():
    return pl.BlockSpec(memory_space=pltpu.MemorySpace.SMEM)


def any_spec():
    return pl.BlockSpec(memory_space=pl.ANY)


def in_vmem(x):
    return pltpu.with_memory_space_constraint(x, VMEM)


def in_hbm(x):
    return pltpu.with_memory_space_constraint(x, pltpu.MemorySpace.HBM)


def cost(flops, nbytes):
    return pl.CostEstimate(flops=flops, bytes_accessed=nbytes, transcendentals=0)


def rim_body(rows, u_ref, v_ref, low_ref, high_ref, sems):
    def copy(k):
        wind, side, d = k // 4, k // 2 % 2, k % 2
        row = d if side == 0 else rows - 2 + d
        return pltpu.make_async_copy(
            (u_ref, v_ref)[wind].at[:, row, :],
            (low_ref, high_ref)[side].at[2 * wind + d],
            sems.at[k],
        )

    for k in range(8):
        copy(k).start()
    for k in range(8):
        copy(k).wait()


def rims(u, v):
    snaps, rows, cols = u.shape
    rim = VMEM((4, snaps, cols), F32)
    return pl.pallas_call(
        functools.partial(rim_body, rows),
        out_shape=(rim, rim),
        in_specs=[any_spec(), any_spec()],
        out_specs=(vmem_spec(),) * 2,
        scratch_shapes=[pltpu.SemaphoreType.DMA((8,))],
        compiler_params=pltpu.CompilerParams(vmem_limit_bytes=1 << 20),
        cost_estimate=cost(0, 1 << 22),
        name="rims",
    )(in_hbm(u), in_hbm(v))


def row_copy(u_ref, v_ref, ut_ref, vt_ref, sems):
    def copy(wind, j):
        src = (u_ref, v_ref)[wind]
        dst = (ut_ref, vt_ref)[wind]
        return pltpu.make_async_copy(src.at[:, j, :], dst.at[j], sems.at[wind, j])

    def start(j, carry):
        copy(0, j).start()
        copy(1, j).start()
        return carry

    return copy, start


def edge_body(rows, u_ref, v_ref, west_ref, east_ref, ut_ref, vt_ref, sems):
    snaps = u_ref.shape[0]
    copy, start = row_copy(u_ref, v_ref, ut_ref, vt_ref, sems)
    lax.fori_loop(0, rows, start, 0)
    step = 32
    lane = lax.broadcasted_iota(jnp.int32, (step, LANES), 1)
    for wind in range(2):
        west_ref[wind] = jnp.zeros((snaps, LANES), F32)
        east_ref[wind] = jnp.zeros((snaps, LANES), F32)

    def pack(i, carry):
        base = i * GROUP
        for k in range(GROUP):
            copy(0, base + k).wait()
            copy(1, base + k).wait()
        for wind in range(2):
            src = (ut_ref, vt_ref)[wind]
            for t in range(0, snaps, step):
                part = pl.ds(t, step)
                west, east = west_ref[wind, part, :], east_ref[wind, part, :]
                for k in range(GROUP):
                    j = base + k
                    turned = pltpu.roll(src[j, part, :], 2 * j + 2, 1)
                    west = jnp.where((lane >> 1) == j + 1, turned, west)
                    east = jnp.where((lane >> 1) == j, turned, east)
                west_ref[wind, part, :] = west
                east_ref[wind, part, :] = east
        return carry

    lax.fori_loop(0, rows // GROUP, pack, 0)


def edges(u, v):
    snaps, rows, cols = u.shape
    packed = VMEM((2, snaps, LANES), F32)
    return pl.pallas_call(
        functools.partial(edge_body, rows),
        out_shape=(packed, packed),
        in_specs=[any_spec(), any_spec()],
        out_specs=(vmem_spec(),) * 2,
        scratch_shapes=[
            pltpu.VMEM((rows, snaps, cols), F32),
            pltpu.VMEM((rows, snaps, cols), F32),
            pltpu.SemaphoreType.DMA((2, rows)),
        ],
        compiler_params=pltpu.CompilerParams(vmem_limit_bytes=16 << 20),
        cost_estimate=cost(u.size * 8, u.size * 8),
        name="edges",
    )(in_hbm(u), in_hbm(v))


def band():
    size = 2 * LANES
    k = lax.broadcasted_iota(jnp.int32, (size, size), 0)
    n = lax.broadcasted_iota(jnp.int32, (size, size), 1)
    inside = jnp.logical_and((k >> 7) == (n >> 7), (k & (LANES - 1)) < LANES - 2)
    d = n - k
    taps = jnp.where(d == 1, 8.0, jnp.where(jnp.logical_or(d == 0, d == 2), -1.0, 0.0))
    return jnp.where(inside, taps, 0.0).astype(BF16)


def split(x):
    hi = x.astype(BF16)
    return hi, (x - hi.astype(F32)).astype(BF16)


def stencil_row(j, coef_ref, band_ref, u_near, v_near, store, snaps, step):
    lon = coef_ref[j, 0]
    lat = [coef_ref[j, 1 + k] for k in range(4)]

    def across(near, part):
        return (lat[1] * near[3](part) - lat[0] * near[1](part)) - (
            lat[3] * near[4](part) - lat[2] * near[0](part)
        )

    for t in range(0, snaps, step):
        part = pl.ds(t, step)
        ahead = []
        for near in (v_near, u_near):
            cells = near[2](part)
            ahead.append(pltpu.roll(cells, LANES - 2, 1) - cells)
        hi, lo = split(jnp.concatenate(ahead, axis=1))
        taps = band_ref[...]
        along = lax.dot_general(
            lo, taps, (((1,), (0,)), ((), ())), preferred_element_type=F32
        ) + lax.dot_general(hi, taps, (((1,), (0,)), ((), ())), preferred_element_type=F32)
        store(part, 0, lon * along[:, :LANES] - across(u_near, part))
        store(part, 1, lon * along[:, LANES:] + across(v_near, part))


def row_of(ref, j):
    return lambda part: ref[j, part, :]


STENCIL_STEP = 128
STENCIL_ROWS = 4


def stencil_body(rows, u_ref, v_ref, coef_ref, x_ref, ut_ref, vt_ref, band_ref, sems):
    snaps = u_ref.shape[0]
    copy, start = row_copy(u_ref, v_ref, ut_ref, vt_ref, sems)
    lax.fori_loop(0, rows, start, 0)
    band_ref[...] = band()

    def arrived(j):
        copy(0, j).wait()
        copy(1, j).wait()

    def middle(i, carry):
        base = 2 + i * STENCIL_ROWS
        for r in range(STENCIL_ROWS):
            arrived(base + r + 2)
        for r in range(STENCIL_ROWS):
            j = base + r

            def store(part, out, value, j=j):
                x_ref[j, part, out * LANES : (out + 1) * LANES] = value

            near = [
                [row_of(ref, j + d) for d in range(-2, 3)] for ref in (ut_ref, vt_ref)
            ]
            stencil_row(j, coef_ref, band_ref, *near, store, snaps, STENCIL_STEP)
        return carry

    for j in range(4):
        arrived(j)
    lax.fori_loop(0, (rows - 4) // STENCIL_ROWS, middle, 0)


def differences(u, v, coef):
    snaps, rows, cols = u.shape
    return pl.pallas_call(
        functools.partial(stencil_body, rows),
        out_shape=VMEM((rows, snaps, 2 * cols), F32),
        in_specs=[any_spec()] * 2 + [smem_spec()],
        out_specs=vmem_spec(),
        scratch_shapes=[
            pltpu.VMEM((rows, snaps, cols), F32),
            pltpu.VMEM((rows, snaps, cols), F32),
            pltpu.VMEM((2 * LANES, 2 * LANES), BF16),
            pltpu.SemaphoreType.DMA((2, rows)),
        ],
        compiler_params=pltpu.CompilerParams(vmem_limit_bytes=18 << 20),
        cost_estimate=cost(u.size * 2048, u.size * 16),
        name="differences",
    )(in_hbm(u), in_hbm(v), coef)


def gram_body(
    rows, x_ref, west_ref, east_ref, from_west_ref, from_east_ref, north_ref, south_ref,
    u_ref, v_ref, scale_ref, coef_ref,
    hi_ref, lo_ref, out_ref,
    fix_ref, acc_ref, rim_ref, xe_ref, band_ref, sems,
):
    snaps = x_ref.shape[1]
    step = 64

    def rim_copy(wind, k):
        row = k if k < 4 else rows - 8 + k
        return pltpu.make_async_copy(
            (u_ref, v_ref)[wind].at[:, row, :], rim_ref.at[wind, k], sems.at[wind, k]
        )

    for k in range(8):
        rim_copy(0, k).start()
        rim_copy(1, k).start()
    lane = lax.broadcasted_iota(jnp.int32, (step, LANES), 1)
    even = lane % 2 == 0
    even_row = (lane // 2) % 2 == 0
    scale = scale_ref[0:1, :]
    for wind in range(2):
        for t in range(0, snaps, step):
            part = pl.ds(t, step)
            left = pltpu.roll(west_ref[wind, part, :], LANES - 2, 1) - from_west_ref[wind, part, :]
            right = pltpu.roll(from_east_ref[wind, part, :], LANES - 2, 1) - east_ref[wind, part, :]
            left = scale * (jnp.where(even, 8.0 * pltpu.roll(left, LANES - 1, 1), 0.0) - left)
            right = scale * (jnp.where(even, 0.0, 8.0 * pltpu.roll(right, 1, 1)) - right)
            right = pltpu.roll(right, LANES - 2, 1)
            fix_ref[wind, 0, part, :] = jnp.where(even_row, left, right)
            fix_ref[wind, 1, part, :] = jnp.where(even_row, right, left)
    acc_ref[...] = jnp.zeros_like(acc_ref)
    outer = jnp.logical_or(lane < 2, lane >= LANES - 2)

    def group(row_list, parities, loads):
        for j, parity, load in zip(row_list, parities, loads):
            shift = (2 * LANES - 2 * j) % LANES
            for out in range(2):
                for t in range(0, snaps, step):
                    part = pl.ds(t, step)
                    fix = pltpu.roll(fix_ref[1 - out, parity, part, :], shift, 1)
                    span = slice(out * LANES, (out + 1) * LANES)
                    x = load(part, span) + jnp.where(outer, fix, 0.0)
                    hi, lo = split(x)
                    hi_ref[j, part, span] = hi
                    lo_ref[j, part, span] = lo
        total = None
        for j in row_list:
            hi = hi_ref[j]
            both = jnp.concatenate([hi, lo_ref[j]], axis=0)
            term = lax.dot_general(
                hi, both, (((1,), (1,)), ((), ())), preferred_element_type=F32
            )
            total = term if total is None else total + term
        acc_ref[...] += total

    def inner_group(i, carry):
        base = 2 + i * GROUP
        js = [base + k for k in range(GROUP)]
        loads = [lambda part, span, j=j: x_ref[j, part, span] for j in js]
        group(js, [k % 2 for k in range(GROUP)], loads)
        return carry

    lax.fori_loop(0, (rows - 4) // GROUP, inner_group, 0)

    band_ref[...] = band()
    for k in range(8):
        rim_copy(0, k).wait()
        rim_copy(1, k).wait()

    def getter(wind, j):
        if j < 0:
            return row_of(north_ref, wind * 2 + j + 2)
        if j >= rows:
            return row_of(south_ref, wind * 2 + j - rows)
        k = j if j < 4 else j - rows + 8
        return lambda part: rim_ref[wind, k, part, :]

    edge_rows = (0, 1, rows - 2, rows - 1)
    for e, j in enumerate(edge_rows):

        def store(part, out, value, e=e):
            xe_ref[e, part, out * LANES : (out + 1) * LANES] = value

        near = [[getter(wind, j + d) for d in range(-2, 3)] for wind in range(2)]
        stencil_row(j, coef_ref, band_ref, *near, store, snaps, STENCIL_STEP)
    loads = [lambda part, span, e=e: xe_ref[e, part, span] for e in range(4)]
    group(list(edge_rows), [j % 2 for j in edge_rows], loads)

    low = acc_ref[:, snaps:]
    gram = acc_ref[:, :snaps] + (low + low.T)
    row = lax.broadcasted_iota(jnp.int32, (HALF, HALF), 0)
    col = lax.broadcasted_iota(jnp.int32, (HALF, HALF), 1)
    first = gram[:HALF, :HALF]
    second = gram[HALF:, HALF:]
    out_ref[0, :HALF, :] = gram[HALF:, :HALF]
    out_ref[1, :HALF, :] = jnp.where(row >= col, first, second)
    diagonal = jnp.sum(jnp.where(row == col, second, 0.0), axis=0, keepdims=True)
    out_ref[0, HALF:, :] = jnp.broadcast_to(diagonal, (8, HALF))
    out_ref[1, HALF:, :] = jnp.zeros((8, HALF), F32)


def partial_gram(x, west, east, from_west, from_east, north, south, u, v, scale, coef):
    rows, snaps, both = x.shape
    halves = VMEM((rows, snaps, both), BF16)
    return pl.pallas_call(
        functools.partial(gram_body, rows),
        out_shape=(halves, halves, VMEM((2, PIECE, HALF), F32)),
        in_specs=[vmem_spec()] * 7 + [any_spec()] * 2 + [vmem_spec(), smem_spec()],
        out_specs=(vmem_spec(),) * 3,
        scratch_shapes=[
            pltpu.VMEM((2, 2, snaps, LANES), F32),
            pltpu.VMEM((snaps, 2 * snaps), F32),
            pltpu.VMEM((2, 8, snaps, LANES), F32),
            pltpu.VMEM((4, snaps, both), F32),
            pltpu.VMEM((both, both), BF16),
            pltpu.SemaphoreType.DMA((2, 8)),
        ],
        compiler_params=pltpu.CompilerParams(vmem_limit_bytes=14 << 20),
        cost_estimate=cost(x.size * 1024, x.size * 8),
        name="partial_gram",
    )(
        *(in_vmem(y) for y in (x, west, east, from_west, from_east, north, south)),
        in_hbm(u), in_hbm(v), scale, coef,
    )


def swap(x, axis, bit):
    count = lax.axis_size(axis)
    return lax.ppermute(x, axis, [(i, i ^ bit) for i in range(count)])


def powers(count):
    bit = 1
    while bit < count:
        yield bit
        bit *= 2


def summed(parts):
    odd = lax.axis_index("lon") % 2 == 1
    mine = jnp.where(odd, parts[1], parts[0])
    other = jnp.where(odd, parts[0], parts[1])
    mine = mine + swap(other, "lon", 1)
    for bit in powers(lax.axis_size("lat")):
        mine = mine + swap(mine, "lat", bit)
    for bit in powers(lax.axis_size("lon")):
        if bit > 1:
            mine = mine + swap(mine, "lon", bit)
    theirs = swap(mine, "lon", 1)
    return jnp.where(odd, theirs, mine), jnp.where(odd, mine, theirs)


def dot_nt(a, b):
    return lax.dot_general(
        a, b, (((1,), (1,)), ((), ())), precision=lax.Precision.HIGHEST, preferred_element_type=F32
    )


def dot_nn(a, b):
    return lax.dot_general(
        a, b, (((1,), (0,)), ((), ())), precision=lax.Precision.HIGHEST, preferred_element_type=F32
    )


def eliminate(matrix, work_ref, right_ref):
    size = matrix.shape[0]
    groups = size // 8
    row = lax.broadcasted_iota(jnp.int32, (8, size), 0)
    col = lax.broadcasted_iota(jnp.int32, (8, size), 1)

    def spread(x, r):
        return jnp.broadcast_to(x[r : r + 1, :], x.shape)

    def columns(x, g):
        return [jnp.broadcast_to(x[:, 8 * g + r : 8 * g + r + 1], x.shape) for r in range(8)]

    work_ref[...] = matrix
    for g in range(groups):
        right_ref[8 * g : 8 * g + 8, :] = jnp.where(col == row + 8 * g, 1.0, 0.0)
    for g in range(groups):
        here = slice(8 * g, 8 * g + 8)
        work, right = work_ref[here, :], right_ref[here, :]
        cols = columns(work, g)
        steps = []
        for r in range(8):
            inverse = 1.0 / spread(cols[r], r)
            across = {c: spread(cols[c], r) for c in range(r + 1, 8)}
            work_row, right_row = spread(work, r), spread(right, r)
            steps.append((inverse, across, work_row, right_row))
            if r < 7:
                factor = jnp.where(row > r, cols[r] * inverse, 0.0)
                for c in range(r + 1, 8):
                    cols[c] = cols[c] - factor * across[c]
                work = work - factor * work_row
                right = right - factor * right_row
        work_ref[here, :] = work
        right_ref[here, :] = right
        for h in range(g + 1, groups):
            there = slice(8 * h, 8 * h + 8)
            work_h, right_h = work_ref[there, :], right_ref[there, :]
            cols_h = columns(work_h, g)
            for r in range(8):
                inverse, across, work_row, right_row = steps[r]
                factor = cols_h[r] * inverse
                for c in range(r + 1, 8):
                    cols_h[c] = cols_h[c] - factor * across[c]
                work_h = work_h - factor * work_row
                right_h = right_h - factor * right_row
            work_ref[there, :] = work_h
            right_ref[there, :] = right_h
    upper, lower = [], []
    for g in range(groups):
        here = slice(8 * g, 8 * g + 8)
        work, right = work_ref[here, :], right_ref[here, :]
        diagonal = jnp.sum(jnp.where(col == row + 8 * g, work, 0.0), axis=1, keepdims=True)
        root = lax.rsqrt(diagonal)
        upper.append(jnp.where(col >= row + 8 * g, work * root, 0.0))
        lower.append(right * root)
    return jnp.concatenate(upper, axis=0), jnp.concatenate(lower, axis=0)


def factor_body(total, corner_ref, mixed_ref, r_ref, hi_ref, lo_ref, work_ref, right_ref):
    inv = 1.0 / total
    row = lax.broadcasted_iota(jnp.int32, (HALF, HALF), 0)
    col = lax.broadcasted_iota(jnp.int32, (HALF, HALF), 1)
    mixed = mixed_ref[:HALF, :] * inv
    corner = corner_ref[:HALF, :] * inv
    diagonal = corner_ref[HALF : HALF + 1, :] * inv
    turned = mixed.T
    first = jnp.where(row >= col, mixed, turned)
    second = jnp.where(row < col, mixed, jnp.where(row > col, turned, diagonal))
    r11, w11 = eliminate(first, work_ref, right_ref)
    l21 = dot_nt(corner, w11)
    r22, w22 = eliminate(second - dot_nt(l21, l21), work_ref, right_ref)
    w21 = -dot_nn(w22, dot_nn(l21, w11))
    zero = jnp.zeros((HALF, HALF), F32)
    r_ref[:HALF, :HALF] = r11
    r_ref[:HALF, HALF:] = l21.T
    r_ref[HALF:, :HALF] = zero
    r_ref[HALF:, HALF:] = r22
    for i, j, w in ((0, 0, w11), (0, 1, zero), (1, 0, w21), (1, 1, w22)):
        part = (slice(i * HALF, (i + 1) * HALF), slice(j * HALF, (j + 1) * HALF))
        hi = w.astype(BF16)
        hi_ref[part] = hi
        lo_ref[part] = (w - hi.astype(F32)).astype(BF16)


def factor(corner, mixed, total):
    snaps = 2 * HALF
    return pl.pallas_call(
        functools.partial(factor_body, total),
        out_shape=(
            VMEM((snaps, snaps), F32),
            VMEM((snaps, snaps), BF16),
            VMEM((snaps, snaps), BF16),
        ),
        in_specs=[vmem_spec()] * 2,
        out_specs=(vmem_spec(),) * 3,
        scratch_shapes=[pltpu.VMEM((HALF, HALF), F32)] * 2,
        compiler_params=pltpu.CompilerParams(vmem_limit_bytes=12 << 20),
        cost_estimate=cost(1 << 26, 1 << 20),
        name="factor",
    )(in_vmem(corner), in_vmem(mixed))


def basis_body(rows, whi_ref, wlo_ref, hi_ref, lo_ref, r_ref, out_ref, r_out_ref, buf_ref, sems, r_sem):
    slots = buf_ref.shape[0]
    cols = out_ref.shape[3]

    def copy(j, slot, part):
        return pltpu.make_async_copy(
            buf_ref.at[slot, :, pl.ds(part * cols, cols)],
            out_ref.at[:, part, j, :],
            sems.at[slot, part],
        )

    pltpu.make_async_copy(r_ref, r_out_ref, r_sem).start()
    weights = jnp.concatenate([whi_ref[...], whi_ref[...], wlo_ref[...]], axis=1)

    def step(j, carry):
        slot = lax.rem(j, slots)

        @pl.when(j >= slots)
        def _():
            copy(j - slots, slot, 0).wait()
            copy(j - slots, slot, 1).wait()

        cells = jnp.concatenate([hi_ref[j], lo_ref[j], hi_ref[j]], axis=0)
        buf_ref[slot] = lax.dot_general(
            weights, cells, (((1,), (0,)), ((), ())), preferred_element_type=F32
        )
        copy(j, slot, 0).start()
        copy(j, slot, 1).start()
        return carry

    lax.fori_loop(0, rows, step, 0)

    def drain(j, carry):
        slot = lax.rem(j, slots)
        copy(j, slot, 0).wait()
        copy(j, slot, 1).wait()
        return carry

    lax.fori_loop(rows - slots, rows, drain, 0)
    pltpu.make_async_copy(r_ref, r_out_ref, r_sem).wait()


def basis(whi, wlo, hi, lo, r):
    rows, snaps, both = hi.shape
    cols = both // 2
    slots = 8
    return pl.pallas_call(
        functools.partial(basis_body, rows),
        out_shape=(
            jax.ShapeDtypeStruct((snaps, 2, rows, cols), F32),
            jax.ShapeDtypeStruct((snaps, snaps), F32),
        ),
        in_specs=[vmem_spec()] * 5,
        out_specs=(any_spec(), any_spec()),
        scratch_shapes=[
            pltpu.VMEM((slots, snaps, both), F32),
            pltpu.SemaphoreType.DMA((slots, 2)),
            pltpu.SemaphoreType.DMA(()),
        ],
        compiler_params=pltpu.CompilerParams(vmem_limit_bytes=8 << 20),
        cost_estimate=cost(hi.size * 1536, hi.size * 8),
        name="basis",
    )(in_vmem(whi), in_vmem(wlo), in_vmem(hi), in_vmem(lo), in_vmem(r))


def on_device(u, v):
    snaps, rows, cols = u.shape
    n_lat = rows * lax.axis_size("lat")
    lat, lon = lax.axis_size("lat"), lax.axis_size("lon")
    n_lon = cols * lon
    ratio = n_lon / (2.0 * n_lat)

    low, high = rims(u, v)
    north = lax.ppermute(high, "lat", [(i, i + 1) for i in range(lat - 1)])
    south = lax.ppermute(low, "lat", [(i + 1, i) for i in range(lat - 1)])
    u, v, _, _ = lax.optimization_barrier((u, v, low, high))

    index = (lax.axis_index("lat") * rows + jnp.arange(-2, rows + 2)).astype(F32)
    cosine = jnp.cos(-jnp.pi / 2 + (index + 0.5) * jnp.pi / n_lat)
    root = 1.0 / (12.0 * jnp.sqrt(cosine[2:-2]))
    along = ratio * root
    coef = jnp.stack(
        [
            along,
            8.0 * cosine[1:-3] * root,
            8.0 * cosine[3:-1] * root,
            cosine[:-4] * root,
            cosine[4:] * root,
        ],
        axis=1,
    )
    scale = jnp.broadcast_to(
        jnp.pad(jnp.repeat(along, 2), (0, LANES - 2 * rows))[None, :], (8, LANES)
    )

    west, east = edges(u, v)
    from_west = lax.ppermute(east, "lon", [(i, (i + 1) % lon) for i in range(lon)])
    from_east = lax.ppermute(west, "lon", [((i + 1) % lon, i) for i in range(lon)])
    x = differences(u, v, coef)
    hi, lo, parts = partial_gram(
        x, west, east, from_west, from_east, north, south, u, v, scale, coef
    )
    corner, mixed = summed(parts)
    r, whi, wlo = factor(corner, mixed, 2.0 * n_lat * n_lon)
    return basis(whi, wlo, hi, lo, r)


def solution(mesh):
    in_specs = (P(None, "lat", "lon"), P(None, "lat", "lon"))
    out_specs = (P(None, None, "lat", "lon"), P())
    return jax.shard_map(
        on_device, mesh=mesh, in_specs=in_specs, out_specs=out_specs, check_vma=False
    )
```

time: 138 us -> 85.8 us (0.62)
  Pallas kernels: 90 us -> 54.1 us
  local copies, waits for them, and re-layouts: 15.5 us -> 0.33 us
    pallas_call x1, Pallas kernels: 34.9 us -> 9.07 us  [factor(): pl.pallas_call(functools.partial(factor_body, total), out_shape=(VMEM((sn...]
    unnamed x9 -> x0, local copies, waits for them, and re-layouts: 11.6 us -> none
    pallas_call x1, Pallas kernels: 17.1 us -> 11 us  [differences(): pl.pallas_call(functools.partial(stencil_body, rows), out_shape=VMEM((row...]
    pallas_call x2 -> x3, Pallas kernels: 29.2 us -> 23.2 us  [the longest x1 14.3 us: basis(): pl.pallas_call(functools.partial(basis_body, rows), out_shape=(jax.ShapeD...]
    another operation x4 -> x2, local copies, waits for them, and re-layouts: 3.61 us -> 0.12 us  [on_device(): jnp.stack([along, 8.0 * cosine[1:-3] * root, 8.0 * cosine[3:-1] * root, c...]
    pallas_call x1, Pallas kernels: 8.79 us -> 10.8 us  [partial_gram(): pl.pallas_call(functools.partial(gram_body, rows), out_shape=(halves, hal...]
  transfers between devices with their start and end apart: 10 -> 10, of which waited for: 6 -> 6; matrix products, arithmetic and copies ran while one was open for 0% -> 1% of each run, Pallas kernels for 23% -> 22%
where the time goes in v2:
time: 85.8 us; the launch traced here: 85.6 us
  Pallas kernels  54.1 us (63%)
  starting transfers between devices  16.9 us (20%)
  waiting for transfers between devices  13.3 us (16%)
    pallas_call x1, Pallas kernels, basis(): pl.pallas_call(functools.partial(basis_body, rows), out_shape=(jax.ShapeD...  14.3 us
    ppermute x6, waiting for transfers between devices, swap(): return lax.ppermute(x, axis, [(i, i ^ bit) for i in range(count)])  13.3 us
    pallas_call x1, Pallas kernels, differences(): pl.pallas_call(functools.partial(stencil_body, rows), out_shape=VMEM((row...  11 us
    pallas_call x1, Pallas kernels, partial_gram(): pl.pallas_call(functools.partial(gram_body, rows), out_shape=(halves, hal...  10.8 us
    pallas_call x1, Pallas kernels, factor(): pl.pallas_call(functools.partial(factor_body, total), out_shape=(VMEM((sn...  9.07 us
    ppermute x6, starting transfers between devices, swap(): return lax.ppermute(x, axis, [(i, i ^ bit) for i in range(count)])  8.16 us
    pallas_call x1, Pallas kernels, edges(): pl.pallas_call(functools.partial(edge_body, rows), out_shape=(packed, pac...  7.48 us
    ppermute x1, starting transfers between devices, on_device(): north = lax.ppermute(high, 'lat', [(i, i + 1) for i in range(lat - 1)])  5.62 us
  transfers between devices with their start and end apart: 10, of which 6 were waited for; matrix products, arithmetic and copies ran while one was open for 1% of the time, Pallas kernels for 22%

profile of v2, /device:TPU:0, one launch (start us, length us, event | category | flops | bytes accessed | tf_op | source)
XLA Modules:
  0.0 85.6 jit_solution(11623356557641545318)
XLA Ops:
  0.6 1.5 %rims.1 = (f32[4,256,128]{2,1,0:T(8,128)S(1)}, f32[4,256,128]{2,1,0:T(8,128)S(1)}) custom-call(f32[256,48,128]{2,1,0:T(8,128)} %u_ref.4, f32[256,48,128]{2,1,0:T(8,128)} %v_ref.4), custom_call_target="tpu_custom_call" | custom-call | bytes 4194304 | tf_op jit(solution)/shard_map/rims/pallas_call | solution.py:62
  2.1 1.3 %collective-permute-start.3 = (f32[4,256,128]{2,1,0:T(8,128)S(1)}, f32[4,256,128]{2,1,0:T(8,128)S(1)}, u32[]{:S(2)}, u32[]{:S(2)}) collective-permute-start(f32[4,256,128]{2,1,0:T(8,128)S(1)} %get-tuple-element.14), channel_id=1, source_target_pairs={{1,0},{2,1},{3,2},{5,4},{6,5},{7,6},{9,8},{10,9},{11,10},{13,12},{... | collective-permute-start | bytes 1572872 | tf_op jit(solution)/shard_map/ppermute | solution.py:577
  3.4 5.6 %collective-permute-start.2 = (f32[4,256,128]{2,1,0:T(8,128)S(1)}, f32[4,256,128]{2,1,0:T(8,128)S(1)}, u32[]{:S(2)}, u32[]{:S(2)}) collective-permute-start(f32[4,256,128]{2,1,0:T(8,128)S(1)} %get-tuple-element.15), channel_id=1, source_target_pairs={{0,1},{1,2},{2,3},{4,5},{5,6},{6,7},{8,9},{9,10},{10,11},{12,13},{... | collective-permute-start | bytes 1572872 | tf_op jit(solution)/shard_map/ppermute | solution.py:576
  9.0 7.5 %edges.1 = (f32[2,256,128]{2,1,0:T(8,128)S(1)}, f32[2,256,128]{2,1,0:T(8,128)S(1)}) custom-call(f32[256,48,128]{2,1,0:T(8,128)} %u_ref.4, f32[256,48,128]{2,1,0:T(8,128)} %v_ref.4), custom_call_target="tpu_custom_call" | custom-call | flops 12582912 | bytes 12582912 | tf_op jit(solution)/shard_map/edges/pallas_call | solution.py:123
  16.5 1.8 %collective-permute-start.1 = (f32[2,256,128]{2,1,0:T(8,128)S(1)}, f32[2,256,128]{2,1,0:T(8,128)S(1)}, u32[]{:S(2)}, u32[]{:S(2)}) collective-permute-start(f32[2,256,128]{2,1,0:T(8,128)S(1)} %get-tuple-element.18.west_ref), channel_id=1, source_target_pairs={{4,0},{8,4},{12,8},{16,12},{20,16},{24,20},{28,24},{0,28},{5,1},{9... | collective-permute-start | bytes 786440 | tf_op jit(solution)/shard_map/ppermute | solution.py:600
  18.3 0.0 collective-permute-start
  18.4 0.1 broadcast_multiply_fusion
  18.5 0.1 multiply_bitcast_fusion
  18.6 0.1 copy.14.coef_ref
  18.7 0.1 broadcast_in_dim.4
  18.7 0.1 reshape.12
  18.9 11.0 %differences.1.x_ref = f32[48,256,256]{2,1,0:T(8,128)S(1)} custom-call(f32[256,48,128]{2,1,0:T(8,128)} %u_ref.4, f32[256,48,128]{2,1,0:T(8,128)} %v_ref.4, f32[48,5]{1,0:T(8,128)S(1)} %copy.14.coef_ref), custom_call_target="tpu_custom_call" | custom-call | flops 3221225472 | bytes 25165824 | tf_op jit(solution)/shard_map/differences/pallas_call | solution.py:219
  29.9 0.0 collective-permute-done.1.from_east_ref
  30.0 0.0 collective-permute-done.from_west_ref
  30.0 0.0 collective-permute-done.3.south_ref
  30.0 0.0 collective-permute-done.2.north_ref
  30.0 10.8 %partial_gram.1 = (bf16[48,256,256]{2,1,0:T(8,128)(2,1)S(1)}, bf16[48,256,256]{2,1,0:T(8,128)(2,1)S(1)}, f32[2,136,128]{2,1,0:T(8,128)S(1)}) custom-call(f32[48,256,256]{2,1,0:T(8,128)S(1)} %differences.1.x_ref, f32[2,256,128]{2,1,0:T(8,128)S(1)} %get-tuple-element.18.west_ref, f32[2,256,128]{2,1,0:T(8,128)S(1)} %get-tuple-element.19.east_ref, ...), custom_call_target="tpu_custom_call" | custom-call | flops 3221225472 | bytes 25165824 | tf_op jit(solution)/shard_map/partial_gram/pallas_call | solution.py:342
  40.8 0.4 collective-permute-start.4
  41.2 0.9 %collective-permute-done.4 = f32[136,128]{1,0:T(8,128)S(1)} collective-permute-done((f32[136,128]{1,0:T(8,128)S(1)}, f32[136,128]{1,0:T(8,128)S(1)}, u32[]{:S(2)}, u32[]{:S(2)}) %collective-permute-start.4) | collective-permute-done | bytes 69664 | tf_op jit(solution)/shard_map/ppermute | solution.py:366
  42.1 1.6 %collective-permute-start.5 = (f32[136,128]{1,0:T(8,128)S(1)}, f32[136,128]{1,0:T(8,128)S(1)}, u32[]{:S(2)}, u32[]{:S(2)}) collective-permute-start(f32[136,128]{1,0:T(8,128)S(1)} %bitcast_add_fusion), channel_id=1, source_target_pairs={{0,1},{1,0},{2,3},{3,2},{4,5},{5,4},{6,7},{7,6},{8,9},{9,8},{10,11... | collective-permute-start | bytes 208904 | tf_op jit(solution)/shard_map/ppermute | solution.py:366
  43.8 2.9 %collective-permute-done.5 = f32[136,128]{1,0:T(8,128)S(1)} collective-permute-done((f32[136,128]{1,0:T(8,128)S(1)}, f32[136,128]{1,0:T(8,128)S(1)}, u32[]{:S(2)}, u32[]{:S(2)}) %collective-permute-start.5) | collective-permute-done | bytes 69664 | tf_op jit(solution)/shard_map/ppermute | solution.py:366
  46.6 2.6 %collective-permute-start.6 = (f32[136,128]{1,0:T(8,128)S(1)}, f32[136,128]{1,0:T(8,128)S(1)}, u32[]{:S(2)}, u32[]{:S(2)}) collective-permute-start(f32[136,128]{1,0:T(8,128)S(1)} %add.55), channel_id=1, source_target_pairs={{0,2},{1,3},{2,0},{3,1},{4,6},{5,7},{6,4},{7,5},{8,10},{9,11},{10,... | collective-permute-start | bytes 208904 | tf_op jit(solution)/shard_map/ppermute | solution.py:366
  49.3 2.9 %collective-permute-done.6 = f32[136,128]{1,0:T(8,128)S(1)} collective-permute-done((f32[136,128]{1,0:T(8,128)S(1)}, f32[136,128]{1,0:T(8,128)S(1)}, u32[]{:S(2)}, u32[]{:S(2)}) %collective-permute-start.6) | collective-permute-done | bytes 69664 | tf_op jit(solution)/shard_map/ppermute | solution.py:366
  52.2 1.8 %collective-permute-start.7 = (f32[136,128]{1,0:T(8,128)S(1)}, f32[136,128]{1,0:T(8,128)S(1)}, u32[]{:S(2)}, u32[]{:S(2)}) collective-permute-start(f32[136,128]{1,0:T(8,128)S(1)} %add.56), channel_id=1, source_target_pairs={{0,8},{4,12},{8,0},{12,4},{16,24},{20,28},{24,16},{28,20},{1,9},{5... | collective-permute-start | bytes 208904 | tf_op jit(solution)/shard_map/ppermute | solution.py:366
  54.0 2.6 %collective-permute-done.7 = f32[136,128]{1,0:T(8,128)S(1)} collective-permute-done((f32[136,128]{1,0:T(8,128)S(1)}, f32[136,128]{1,0:T(8,128)S(1)}, u32[]{:S(2)}, u32[]{:S(2)}) %collective-permute-start.7) | collective-permute-done | bytes 69664 | tf_op jit(solution)/shard_map/ppermute | solution.py:366
  56.6 1.6 %collective-permute-start.8 = (f32[136,128]{1,0:T(8,128)S(1)}, f32[136,128]{1,0:T(8,128)S(1)}, u32[]{:S(2)}, u32[]{:S(2)}) collective-permute-start(f32[136,128]{1,0:T(8,128)S(1)} %add.57), channel_id=1, source_target_pairs={{0,16},{4,20},{8,24},{12,28},{16,0},{20,4},{24,8},{28,12},{1,17},{... | collective-permute-start | bytes 208904 | tf_op jit(solution)/shard_map/ppermute | solution.py:366
  58.2 2.8 %collective-permute-done.8 = f32[136,128]{1,0:T(8,128)S(1)} collective-permute-done((f32[136,128]{1,0:T(8,128)S(1)}, f32[136,128]{1,0:T(8,128)S(1)}, u32[]{:S(2)}, u32[]{:S(2)}) %collective-permute-start.8) | collective-permute-done | bytes 69664 | tf_op jit(solution)/shard_map/ppermute | solution.py:366
  61.0 0.1 collective-permute-start.9
  61.0 1.2 %collective-permute-done.9 = f32[136,128]{1,0:T(8,128)S(1)} collective-permute-done((f32[136,128]{1,0:T(8,128)S(1)}, f32[136,128]{1,0:T(8,128)S(1)}, u32[]{:S(2)}, u32[]{:S(2)}) %collective-permute-start.9) | collective-permute-done | bytes 69664 | tf_op jit(solution)/shard_map/ppermute | solution.py:366
  62.3 9.1 %factor.1 = (f32[256,256]{1,0:T(8,128)S(1)}, bf16[256,256]{1,0:T(8,128)(2,1)S(1)}, bf16[256,256]{1,0:T(8,128)(2,1)S(1)}) custom-call(f32[136,128]{1,0:T(8,128)S(1)} %get-tuple-element.29.corner_ref, f32[136,128]{1,0:T(8,128)S(1)} %get-tuple-element.28.mixed_ref), custom_call_target="tpu_custom_call" | custom-call | flops 67108864 | bytes 1048576 | tf_op jit(solution)/shard_map/factor/pallas_call | solution.py:487
  71.4 14.3 %basis.1 = (f32[256,2,48,128]{3,2,1,0:T(8,128)}, f32[256,256]{1,0:T(8,128)}) custom-call(bf16[256,256]{1,0:T(8,128)(2,1)S(1)} %get-tuple-element.21.whi_ref, bf16[256,256]{1,0:T(8,128)(2,1)S(1)} %get-tuple-element.22.wlo_ref, bf16[48,256,256]{2,1,0:T(8,128)(2,1)S(1)} %get-tuple-element.23.hi_ref, bf16[48,256,256]{2,1,0:T(8,128)(2,1)S(1)} %get-tuple-element.24.lo_ref, ...), custom_call_target="tpu_custom_call" | custom-call | flops 4831838208 | bytes 25165824 | tf_op jit(solution)/shard_map/basis/pallas_call | solution.py:549
  (11 shorter events, 0.2 us)
Async XLA Ops:
  2.1 27.9 %collective-permute-start.3 = (f32[4,256,128]{2,1,0:T(8,128)S(1)}, f32[4,256,128]{2,1,0:T(8,128)S(1)}, u32[]{:S(2)}, u32[]{:S(2)}) collective-permute-start(f32[4,256,128]{2,1,0:T(8,128)S(1)} %get-tuple-element.14), channel_id=1, source_target_pairs={{1,0},{2,1},{3,2},{5,4},{6,5},{7,6},{9,8},{10,9},{11,10},{13,12},{... | collective-permute-start | bytes 1572872 | tf_op jit(solution)/shard_map/ppermute | solution.py:577
  3.4 26.6 %collective-permute-start.2 = (f32[4,256,128]{2,1,0:T(8,128)S(1)}, f32[4,256,128]{2,1,0:T(8,128)S(1)}, u32[]{:S(2)}, u32[]{:S(2)}) collective-permute-start(f32[4,256,128]{2,1,0:T(8,128)S(1)} %get-tuple-element.15), channel_id=1, source_target_pairs={{0,1},{1,2},{2,3},{4,5},{5,6},{6,7},{8,9},{9,10},{10,11},{12,13},{... | collective-permute-start | bytes 1572872 | tf_op jit(solution)/shard_map/ppermute | solution.py:576
  16.5 13.4 %collective-permute-start.1 = (f32[2,256,128]{2,1,0:T(8,128)S(1)}, f32[2,256,128]{2,1,0:T(8,128)S(1)}, u32[]{:S(2)}, u32[]{:S(2)}) collective-permute-start(f32[2,256,128]{2,1,0:T(8,128)S(1)} %get-tuple-element.18.west_ref), channel_id=1, source_target_pairs={{4,0},{8,4},{12,8},{16,12},{20,16},{24,20},{28,24},{0,28},{5,1},{9... | collective-permute-start | bytes 786440 | tf_op jit(solution)/shard_map/ppermute | solution.py:600
  18.3 11.6 %collective-permute-start = (f32[2,256,128]{2,1,0:T(8,128)S(1)}, f32[2,256,128]{2,1,0:T(8,128)S(1)}, u32[]{:S(2)}, u32[]{:S(2)}) collective-permute-start(f32[2,256,128]{2,1,0:T(8,128)S(1)} %get-tuple-element.19.east_ref), channel_id=1, source_target_pairs={{0,4},{4,8},{8,12},{12,16},{16,20},{20,24},{24,28},{28,0},{1,5},{5... | collective-permute-start | bytes 786440 | tf_op jit(solution)/shard_map/ppermute | solution.py:599
  40.8 1.3 %collective-permute-start.4 = (f32[136,128]{1,0:T(8,128)S(1)}, f32[136,128]{1,0:T(8,128)S(1)}, u32[]{:S(2)}, u32[]{:S(2)}) collective-permute-start(f32[136,128]{1,0:T(8,128)S(1)} %select_bitcast_fusion), channel_id=1, source_target_pairs={{0,4},{4,0},{8,12},{12,8},{16,20},{20,16},{24,28},{28,24},{1,5},{5... | collective-permute-start | bytes 208904 | tf_op jit(solution)/shard_map/ppermute | solution.py:366
  42.1 4.5 %collective-permute-start.5 = (f32[136,128]{1,0:T(8,128)S(1)}, f32[136,128]{1,0:T(8,128)S(1)}, u32[]{:S(2)}, u32[]{:S(2)}) collective-permute-start(f32[136,128]{1,0:T(8,128)S(1)} %bitcast_add_fusion), channel_id=1, source_target_pairs={{0,1},{1,0},{2,3},{3,2},{4,5},{5,4},{6,7},{7,6},{8,9},{9,8},{10,11... | collective-permute-start | bytes 208904 | tf_op jit(solution)/shard_map/ppermute | solution.py:366
  46.6 5.5 %collective-permute-start.6 = (f32[136,128]{1,0:T(8,128)S(1)}, f32[136,128]{1,0:T(8,128)S(1)}, u32[]{:S(2)}, u32[]{:S(2)}) collective-permute-start(f32[136,128]{1,0:T(8,128)S(1)} %add.55), channel_id=1, source_target_pairs={{0,2},{1,3},{2,0},{3,1},{4,6},{5,7},{6,4},{7,5},{8,10},{9,11},{10,... | collective-permute-start | bytes 208904 | tf_op jit(solution)/shard_map/ppermute | solution.py:366
  52.2 4.4 %collective-permute-start.7 = (f32[136,128]{1,0:T(8,128)S(1)}, f32[136,128]{1,0:T(8,128)S(1)}, u32[]{:S(2)}, u32[]{:S(2)}) collective-permute-start(f32[136,128]{1,0:T(8,128)S(1)} %add.56), channel_id=1, source_target_pairs={{0,8},{4,12},{8,0},{12,4},{16,24},{20,28},{24,16},{28,20},{1,9},{5... | collective-permute-start | bytes 208904 | tf_op jit(solution)/shard_map/ppermute | solution.py:366
  56.6 4.4 %collective-permute-start.8 = (f32[136,128]{1,0:T(8,128)S(1)}, f32[136,128]{1,0:T(8,128)S(1)}, u32[]{:S(2)}, u32[]{:S(2)}) collective-permute-start(f32[136,128]{1,0:T(8,128)S(1)} %add.57), channel_id=1, source_target_pairs={{0,16},{4,20},{8,24},{12,28},{16,0},{20,4},{24,8},{28,12},{1,17},{... | collective-permute-start | bytes 208904 | tf_op jit(solution)/shard_map/ppermute | solution.py:366
  61.0 1.3 %collective-permute-start.9 = (f32[136,128]{1,0:T(8,128)S(1)}, f32[136,128]{1,0:T(8,128)S(1)}, u32[]{:S(2)}, u32[]{:S(2)}) collective-permute-start(f32[136,128]{1,0:T(8,128)S(1)} %add.58), channel_id=1, source_target_pairs={{0,4},{4,0},{8,12},{12,8},{16,20},{20,16},{24,28},{28,24},{1,5},{5... | collective-permute-start | bytes 208904 | tf_op jit(solution)/shard_map/ppermute | solution.py:366

commit v3 on v2

--- a/solution.py
+++ b/solution.py
@@ -2,6 +2,7 @@
 
 import jax
 import jax.numpy as jnp
+import numpy as np
 from jax import lax
 from jax.experimental import pallas as pl
 from jax.experimental.pallas import tpu as pltpu
@@ -14,6 +15,7 @@
 HALF = 128
 PIECE = HALF + 8
 GROUP = 4
+GRAM_ROWS = 22
 
 
 def vmem_spec():
@@ -85,21 +87,90 @@
     return copy, start
 
 
-def edge_body(rows, u_ref, v_ref, west_ref, east_ref, ut_ref, vt_ref, sems):
+TABLE = 1024
+TAPS = 5
+
+
+def table_copy(table_ref, coef_ref, sem):
+    here = pl.multiple_of(lax.axis_index("lat") * TABLE, TABLE)
+    return pltpu.make_async_copy(table_ref.at[pl.ds(here, TABLE)], coef_ref, sem)
+
+
+def band():
+    size = 2 * LANES
+    k = lax.broadcasted_iota(jnp.int32, (size, size), 0)
+    n = lax.broadcasted_iota(jnp.int32, (size, size), 1)
+    inside = jnp.logical_and((k >> 7) == (n >> 7), (k & (LANES - 1)) < LANES - 2)
+    d = n - k
+    taps = jnp.where(d == 1, 8.0, jnp.where(jnp.logical_or(d == 0, d == 2), -1.0, 0.0))
+    return jnp.where(inside, taps, 0.0).astype(BF16)
+
+
+def split(x):
+    hi = x.astype(BF16)
+    return hi, (x - hi.astype(F32)).astype(BF16)
+
+
+def stencil_row(j, coef_ref, band_ref, u_near, v_near, store, snaps, step):
+    lon, *lat = [coef_ref[TAPS * j + k] for k in range(TAPS)]
+
+    def across(near, part):
+        return (lat[1] * near[3](part) - lat[0] * near[1](part)) - (
+            lat[3] * near[4](part) - lat[2] * near[0](part)
+        )
+
+    for t in range(0, snaps, step):
+        part = pl.ds(t, step)
+        ahead = []
+        for near in (v_near, u_near):
+            cells = near[2](part)
+            ahead.append(pltpu.roll(cells, LANES - 2, 1) - cells)
+        hi, lo = split(jnp.concatenate(ahead, axis=1))
+        both = lax.dot_general(
+            jnp.concatenate([lo, hi], axis=0),
+            band_ref[...],
+            (((1,), (0,)), ((), ())),
+            preferred_element_type=F32,
+        )
+        along = both[:step] + both[step:]
+        store(part, 0, lon * along[:, :LANES] - across(u_near, part))
+        store(part, 1, lon * along[:, LANES:] + across(v_near, part))
+
+
+def row_of(ref, j):
+    return lambda part: ref[j, part, :]
+
+
+def store_row(x_ref, j):
+    def store(part, out, value):
+        x_ref[j, part, out * LANES : (out + 1) * LANES] = value
+
+    return store
+
+
+def near_rows(ut_ref, vt_ref, j):
+    return [[row_of(ref, j + d) for d in range(-2, 3)] for ref in (ut_ref, vt_ref)]
+
+
+STENCIL_STEP = 128
+
+
+def edge_body(
+    rows, u_ref, v_ref, lanes_ref, west_ref, east_ref, scale_ref, ut_ref, vt_ref, sems, extra
+):
     snaps = u_ref.shape[0]
     copy, start = row_copy(u_ref, v_ref, ut_ref, vt_ref, sems)
-    lax.fori_loop(0, rows, start, 0)
+    lax.fori_loop(0, GROUP, start, 0)
+    get_scale = pltpu.make_async_copy(lanes_ref.at[lax.axis_index("lat")], scale_ref, extra)
+    get_scale.start()
+    lax.fori_loop(GROUP, rows, start, 0)
     step = 32
     lane = lax.broadcasted_iota(jnp.int32, (step, LANES), 1)
     for wind in range(2):
         west_ref[wind] = jnp.zeros((snaps, LANES), F32)
         east_ref[wind] = jnp.zeros((snaps, LANES), F32)
 
-    def pack(i, carry):
-        base = i * GROUP
-        for k in range(GROUP):
-            copy(0, base + k).wait()
-            copy(1, base + k).wait()
+    def pack(base):
         for wind in range(2):
             src = (ut_ref, vt_ref)[wind]
             for t in range(0, snaps, step):
@@ -112,81 +183,55 @@
                     east = jnp.where((lane >> 1) == j, turned, east)
                 west_ref[wind, part, :] = west
                 east_ref[wind, part, :] = east
+
+    def arrived(base):
+        for k in range(GROUP):
+            copy(0, base + k).wait()
+            copy(1, base + k).wait()
+
+    def body(i, carry):
+        arrived(i * GROUP)
+        pack(i * GROUP)
         return carry
 
-    lax.fori_loop(0, rows // GROUP, pack, 0)
-
-
-def edges(u, v):
+    lax.fori_loop(0, rows // GROUP, body, 0)
+    get_scale.wait()
+
+
+def edges(u, v, lanes):
     snaps, rows, cols = u.shape
     packed = VMEM((2, snaps, LANES), F32)
     return pl.pallas_call(
         functools.partial(edge_body, rows),
-        out_shape=(packed, packed),
-        in_specs=[any_spec(), any_spec()],
-        out_specs=(vmem_spec(),) * 2,
+        out_shape=(packed, packed, VMEM((8, LANES), F32)),
+        in_specs=[any_spec()] * 3,
+        out_specs=(vmem_spec(),) * 3,
         scratch_shapes=[
             pltpu.VMEM((rows, snaps, cols), F32),
             pltpu.VMEM((rows, snaps, cols), F32),
             pltpu.SemaphoreType.DMA((2, rows)),
+            pltpu.SemaphoreType.DMA(()),
         ],
         compiler_params=pltpu.CompilerParams(vmem_limit_bytes=16 << 20),
         cost_estimate=cost(u.size * 8, u.size * 8),
         name="edges",
-    )(in_hbm(u), in_hbm(v))
-
-
-def band():
-    size = 2 * LANES
-    k = lax.broadcasted_iota(jnp.int32, (size, size), 0)
-    n = lax.broadcasted_iota(jnp.int32, (size, size), 1)
-    inside = jnp.logical_and((k >> 7) == (n >> 7), (k & (LANES - 1)) < LANES - 2)
-    d = n - k
-    taps = jnp.where(d == 1, 8.0, jnp.where(jnp.logical_or(d == 0, d == 2), -1.0, 0.0))
-    return jnp.where(inside, taps, 0.0).astype(BF16)
-
-
-def split(x):
-    hi = x.astype(BF16)
-    return hi, (x - hi.astype(F32)).astype(BF16)
-
-
-def stencil_row(j, coef_ref, band_ref, u_near, v_near, store, snaps, step):
-    lon = coef_ref[j, 0]
-    lat = [coef_ref[j, 1 + k] for k in range(4)]
-
-    def across(near, part):
-        return (lat[1] * near[3](part) - lat[0] * near[1](part)) - (
-            lat[3] * near[4](part) - lat[2] * near[0](part)
-        )
-
-    for t in range(0, snaps, step):
-        part = pl.ds(t, step)
-        ahead = []
-        for near in (v_near, u_near):
-            cells = near[2](part)
-            ahead.append(pltpu.roll(cells, LANES - 2, 1) - cells)
-        hi, lo = split(jnp.concatenate(ahead, axis=1))
-        taps = band_ref[...]
-        along = lax.dot_general(
-            lo, taps, (((1,), (0,)), ((), ())), preferred_element_type=F32
-        ) + lax.dot_general(hi, taps, (((1,), (0,)), ((), ())), preferred_element_type=F32)
-        store(part, 0, lon * along[:, :LANES] - across(u_near, part))
-        store(part, 1, lon * along[:, LANES:] + across(v_near, part))
-
-
-def row_of(ref, j):
-    return lambda part: ref[j, part, :]
-
-
-STENCIL_STEP = 128
+    )(in_hbm(u), in_hbm(v), in_hbm(lanes))
+
+
 STENCIL_ROWS = 4
 
 
-def stencil_body(rows, u_ref, v_ref, coef_ref, x_ref, ut_ref, vt_ref, band_ref, sems):
+def stencil_body(
+    rows, u_ref, v_ref, table_ref, x_ref,
+    ut_ref, vt_ref, band_ref, coef_ref, sems, extra,
+):
     snaps = u_ref.shape[0]
+    first = 2
     copy, start = row_copy(u_ref, v_ref, ut_ref, vt_ref, sems)
-    lax.fori_loop(0, rows, start, 0)
+    get_coef = table_copy(table_ref, coef_ref, extra)
+    lax.fori_loop(first - 2, first + 2, start, 0)
+    get_coef.start()
+    lax.fori_loop(first + 2, rows, start, 0)
     band_ref[...] = band()
 
     def arrived(j):
@@ -194,50 +239,49 @@
         copy(1, j).wait()
 
     def middle(i, carry):
-        base = 2 + i * STENCIL_ROWS
+        base = first + i * STENCIL_ROWS
         for r in range(STENCIL_ROWS):
             arrived(base + r + 2)
         for r in range(STENCIL_ROWS):
             j = base + r
-
-            def store(part, out, value, j=j):
-                x_ref[j, part, out * LANES : (out + 1) * LANES] = value
-
-            near = [
-                [row_of(ref, j + d) for d in range(-2, 3)] for ref in (ut_ref, vt_ref)
-            ]
-            stencil_row(j, coef_ref, band_ref, *near, store, snaps, STENCIL_STEP)
+            near = near_rows(ut_ref, vt_ref, j)
+            stencil_row(
+                j, coef_ref, band_ref, *near, store_row(x_ref, j - first), snaps, STENCIL_STEP
+            )
         return carry
 
-    for j in range(4):
+    for j in range(first - 2, first + 2):
         arrived(j)
+    get_coef.wait()
     lax.fori_loop(0, (rows - 4) // STENCIL_ROWS, middle, 0)
 
 
-def differences(u, v, coef):
+def differences(u, v, table):
     snaps, rows, cols = u.shape
     return pl.pallas_call(
         functools.partial(stencil_body, rows),
-        out_shape=VMEM((rows, snaps, 2 * cols), F32),
-        in_specs=[any_spec()] * 2 + [smem_spec()],
+        out_shape=VMEM((rows - 4, snaps, 2 * cols), F32),
+        in_specs=[any_spec()] * 3,
         out_specs=vmem_spec(),
         scratch_shapes=[
             pltpu.VMEM((rows, snaps, cols), F32),
             pltpu.VMEM((rows, snaps, cols), F32),
             pltpu.VMEM((2 * LANES, 2 * LANES), BF16),
+            pltpu.SMEM((TABLE,), F32),
             pltpu.SemaphoreType.DMA((2, rows)),
+            pltpu.SemaphoreType.DMA(()),
         ],
         compiler_params=pltpu.CompilerParams(vmem_limit_bytes=18 << 20),
         cost_estimate=cost(u.size * 2048, u.size * 16),
         name="differences",
-    )(in_hbm(u), in_hbm(v), coef)
+    )(in_hbm(u), in_hbm(v), in_hbm(table))
 
 
 def gram_body(
     rows, x_ref, west_ref, east_ref, from_west_ref, from_east_ref, north_ref, south_ref,
-    u_ref, v_ref, scale_ref, coef_ref,
+    scale_ref, u_ref, v_ref, table_ref,
     hi_ref, lo_ref, out_ref,
-    fix_ref, acc_ref, rim_ref, xe_ref, band_ref, sems,
+    fix_ref, acc_ref, rim_ref, xe_ref, band_ref, coef_ref, sems, extra,
 ):
     snaps = x_ref.shape[1]
     step = 64
@@ -248,6 +292,8 @@
             (u_ref, v_ref)[wind].at[:, row, :], rim_ref.at[wind, k], sems.at[wind, k]
         )
 
+    get_coef = table_copy(table_ref, coef_ref, extra)
+    get_coef.start()
     for k in range(8):
         rim_copy(0, k).start()
         rim_copy(1, k).start()
@@ -291,15 +337,18 @@
         acc_ref[...] += total
 
     def inner_group(i, carry):
-        base = 2 + i * GROUP
-        js = [base + k for k in range(GROUP)]
-        loads = [lambda part, span, j=j: x_ref[j, part, span] for j in js]
-        group(js, [k % 2 for k in range(GROUP)], loads)
+        base = i * GRAM_ROWS
+        loads = [
+            lambda part, span, k=base + k: x_ref[k, part, span] for k in range(GRAM_ROWS)
+        ]
+        js = [base + k + 2 for k in range(GRAM_ROWS)]
+        group(js, [k % 2 for k in range(GRAM_ROWS)], loads)
         return carry
 
-    lax.fori_loop(0, (rows - 4) // GROUP, inner_group, 0)
+    lax.fori_loop(0, (rows - 4) // GRAM_ROWS, inner_group, 0)
 
     band_ref[...] = band()
+    get_coef.wait()
     for k in range(8):
         rim_copy(0, k).wait()
         rim_copy(1, k).wait()
@@ -314,12 +363,8 @@
 
     edge_rows = (0, 1, rows - 2, rows - 1)
     for e, j in enumerate(edge_rows):
-
-        def store(part, out, value, e=e):
-            xe_ref[e, part, out * LANES : (out + 1) * LANES] = value
-
         near = [[getter(wind, j + d) for d in range(-2, 3)] for wind in range(2)]
-        stencil_row(j, coef_ref, band_ref, *near, store, snaps, STENCIL_STEP)
+        stencil_row(j, coef_ref, band_ref, *near, store_row(xe_ref, e), snaps, STENCIL_STEP)
     loads = [lambda part, span, e=e: xe_ref[e, part, span] for e in range(4)]
     group(list(edge_rows), [j % 2 for j in edge_rows], loads)
 
@@ -336,13 +381,14 @@
     out_ref[1, HALF:, :] = jnp.zeros((8, HALF), F32)
 
 
-def partial_gram(x, west, east, from_west, from_east, north, south, u, v, scale, coef):
-    rows, snaps, both = x.shape
+def partial_gram(x, west, east, from_west, from_east, north, south, scale, u, v, table):
+    snaps, rows, cols = u.shape
+    both = 2 * cols
     halves = VMEM((rows, snaps, both), BF16)
     return pl.pallas_call(
         functools.partial(gram_body, rows),
         out_shape=(halves, halves, VMEM((2, PIECE, HALF), F32)),
-        in_specs=[vmem_spec()] * 7 + [any_spec()] * 2 + [vmem_spec(), smem_spec()],
+        in_specs=[vmem_spec()] * 8 + [any_spec()] * 3,
         out_specs=(vmem_spec(),) * 3,
         scratch_shapes=[
             pltpu.VMEM((2, 2, snaps, LANES), F32),
@@ -350,14 +396,19 @@
             pltpu.VMEM((2, 8, snaps, LANES), F32),
             pltpu.VMEM((4, snaps, both), F32),
             pltpu.VMEM((both, both), BF16),
+            pltpu.SMEM((TABLE,), F32),
             pltpu.SemaphoreType.DMA((2, 8)),
+            pltpu.SemaphoreType.DMA(()),
         ],
         compiler_params=pltpu.CompilerParams(vmem_limit_bytes=14 << 20),
-        cost_estimate=cost(x.size * 1024, x.size * 8),
+        cost_estimate=cost(u.size * 2048, u.size * 16),
         name="partial_gram",
     )(
-        *(in_vmem(y) for y in (x, west, east, from_west, from_east, north, south)),
-        in_hbm(u), in_hbm(v), scale, coef,
+        *(
+            in_vmem(y)
+            for y in (x, west, east, from_west, from_east, north, south, scale)
+        ),
+        in_hbm(u), in_hbm(v), in_hbm(table),
     )
 
 
@@ -366,11 +417,23 @@
     return lax.ppermute(x, axis, [(i, i ^ bit) for i in range(count)])
 
 
-def powers(count):
-    bit = 1
-    while bit < count:
-        yield bit
-        bit *= 2
+def bits_from(first, count):
+    bits = []
+    while first < count:
+        bits.append(first)
+        first *= 2
+    return bits
+
+
+def summed_over(x, axis, bits):
+    while bits:
+        if len(bits) > 1:
+            one, two, bits = bits[0], bits[1], bits[2:]
+            near, far, both = (swap(x, axis, b) for b in (one, two, one + two))
+            x = (x + near) + (far + both)
+        else:
+            x, bits = x + swap(x, axis, bits[0]), []
+    return x
 
 
 def summed(parts):
@@ -378,11 +441,8 @@
     mine = jnp.where(odd, parts[1], parts[0])
     other = jnp.where(odd, parts[0], parts[1])
     mine = mine + swap(other, "lon", 1)
-    for bit in powers(lax.axis_size("lat")):
-        mine = mine + swap(mine, "lat", bit)
-    for bit in powers(lax.axis_size("lon")):
-        if bit > 1:
-            mine = mine + swap(mine, "lon", bit)
+    mine = summed_over(mine, "lon", bits_from(2, lax.axis_size("lon")))
+    mine = summed_over(mine, "lat", bits_from(1, lax.axis_size("lat")))
     theirs = swap(mine, "lon", 1)
     return jnp.where(odd, theirs, mine), jnp.where(odd, mine, theirs)
 
@@ -420,7 +480,7 @@
         cols = columns(work, g)
         steps = []
         for r in range(8):
-            inverse = 1.0 / spread(cols[r], r)
+            inverse = spread(1.0 / cols[r], r)
             across = {c: spread(cols[c], r) for c in range(r + 1, 8)}
             work_row, right_row = spread(work, r), spread(right, r)
             steps.append((inverse, across, work_row, right_row))
@@ -512,25 +572,30 @@
         )
 
     pltpu.make_async_copy(r_ref, r_out_ref, r_sem).start()
-    weights = jnp.concatenate([whi_ref[...], whi_ref[...], wlo_ref[...]], axis=1)
-
-    def step(j, carry):
-        slot = lax.rem(j, slots)
-
-        @pl.when(j >= slots)
-        def _():
-            copy(j - slots, slot, 0).wait()
-            copy(j - slots, slot, 1).wait()
-
-        cells = jnp.concatenate([hi_ref[j], lo_ref[j], hi_ref[j]], axis=0)
-        buf_ref[slot] = lax.dot_general(
-            weights, cells, (((1,), (0,)), ((), ())), preferred_element_type=F32
-        )
-        copy(j, slot, 0).start()
-        copy(j, slot, 1).start()
+    full, top = jnp.concatenate([whi_ref[...], wlo_ref[...]], axis=0), whi_ref[...]
+    snaps = top.shape[0]
+
+    def dot(a, b):
+        return lax.dot_general(a, b, (((1,), (0,)), ((), ())), preferred_element_type=F32)
+
+    def step(i, carry):
+        js = [i * BASIS_ROWS + k for k in range(BASIS_ROWS)]
+        for j in js:
+
+            @pl.when(j >= slots)
+            def _(j=j):
+                for part in range(2):
+                    copy(j - slots, lax.rem(j, slots), part).wait()
+
+        for j in js:
+            main = dot(full, hi_ref[j])
+            buf_ref[lax.rem(j, slots)] = main[:snaps] + (main[snaps:] + dot(top, lo_ref[j]))
+        for j in js:
+            for part in range(2):
+                copy(j, lax.rem(j, slots), part).start()
         return carry
 
-    lax.fori_loop(0, rows, step, 0)
+    lax.fori_loop(0, rows // BASIS_ROWS, step, 0)
 
     def drain(j, carry):
         slot = lax.rem(j, slots)
@@ -542,10 +607,13 @@
     pltpu.make_async_copy(r_ref, r_out_ref, r_sem).wait()
 
 
+BASIS_ROWS = 8
+
+
 def basis(whi, wlo, hi, lo, r):
     rows, snaps, both = hi.shape
     cols = both // 2
-    slots = 8
+    slots = 2 * BASIS_ROWS
     return pl.pallas_call(
         functools.partial(basis_body, rows),
         out_shape=(
@@ -577,11 +645,11 @@
     south = lax.ppermute(low, "lat", [(i + 1, i) for i in range(lat - 1)])
     u, v, _, _ = lax.optimization_barrier((u, v, low, high))
 
-    index = (lax.axis_index("lat") * rows + jnp.arange(-2, rows + 2)).astype(F32)
-    cosine = jnp.cos(-jnp.pi / 2 + (index + 0.5) * jnp.pi / n_lat)
-    root = 1.0 / (12.0 * jnp.sqrt(cosine[2:-2]))
+    index = np.arange(-2, n_lat + 2, dtype=np.float64)
+    cosine = np.cos(-np.pi / 2 + (index + 0.5) * np.pi / n_lat)
+    root = 1.0 / (12.0 * np.sqrt(cosine[2:-2]))
     along = ratio * root
-    coef = jnp.stack(
+    table = np.stack(
         [
             along,
             8.0 * cosine[1:-3] * root,
@@ -590,17 +658,18 @@
             cosine[4:] * root,
         ],
         axis=1,
-    )
-    scale = jnp.broadcast_to(
-        jnp.pad(jnp.repeat(along, 2), (0, LANES - 2 * rows))[None, :], (8, LANES)
-    )
-
-    west, east = edges(u, v)
+    ).reshape(lat, rows * TAPS)
+    table = jnp.asarray(np.pad(table, ((0, 0), (0, TABLE - rows * TAPS))).reshape(-1), F32)
+    lanes = np.zeros((lat, 8, LANES))
+    lanes[:, :, : 2 * rows] = np.repeat(along.reshape(lat, rows), 2, axis=1)[:, None, :]
+    lanes = jnp.asarray(lanes, F32)
+
+    west, east, scale = edges(u, v, lanes)
     from_west = lax.ppermute(east, "lon", [(i, (i + 1) % lon) for i in range(lon)])
     from_east = lax.ppermute(west, "lon", [((i + 1) % lon, i) for i in range(lon)])
-    x = differences(u, v, coef)
+    x = differences(u, v, table)
     hi, lo, parts = partial_gram(
-        x, west, east, from_west, from_east, north, south, u, v, scale, coef
+        x, west, east, from_west, from_east, north, south, scale, u, v, table
     )
     corner, mixed = summed(parts)
     r, whi, wlo = factor(corner, mixed, 2.0 * n_lat * n_lon)

time: 85.8 us -> 73.6 us (0.86)
  Pallas kernels: 54.1 us -> 43.6 us
  waiting for transfers between devices: 13.3 us -> 10.9 us
  starting transfers between devices: 16.9 us -> 18 us
    pallas_call x1, Pallas kernels: 14.3 us -> 8.77 us  [basis(): pl.pallas_call(functools.partial(basis_body, rows), out_shape=(jax.ShapeD...]
    pallas_call x1, Pallas kernels: 10.8 us -> 7.36 us  [partial_gram(): pl.pallas_call(functools.partial(gram_body, rows), out_shape=(halves, hal...]
    ppermute x6 -> x8, waiting for transfers between devices: 13.3 us -> 10.9 us  [swap(): return lax.ppermute(x, axis, [(i, i ^ bit) for i in range(count)])]
    pallas_call x1, Pallas kernels: 11 us -> 9.66 us  [differences(): pl.pallas_call(functools.partial(stencil_body, rows), out_shape=VMEM((row...]
    ppermute x6 -> x8, starting transfers between devices: 8.16 us -> 9.07 us  [swap(): return lax.ppermute(x, axis, [(i, i ^ bit) for i in range(count)])]
  transfers between devices with their start and end apart: 10 -> 12, of which waited for: 6 -> 8; matrix products, arithmetic and copies ran while one was open for 1% -> 0% of each run, Pallas kernels for 22% -> 23%
where the time goes in v3:
time: 73.6 us; the launch traced here: 73.4 us
  Pallas kernels  43.6 us (59%)
  starting transfers between devices  18 us (24%)
  waiting for transfers between devices  10.9 us (15%)
  between operations  0.76 us (1%)
    ppermute x8, waiting for transfers between devices, swap(): return lax.ppermute(x, axis, [(i, i ^ bit) for i in range(count)])  10.9 us
    pallas_call x1, Pallas kernels, differences(): pl.pallas_call(functools.partial(stencil_body, rows), out_shape=VMEM((row...  9.66 us
    ppermute x8, starting transfers between devices, swap(): return lax.ppermute(x, axis, [(i, i ^ bit) for i in range(count)])  9.07 us
    pallas_call x1, Pallas kernels, factor(): pl.pallas_call(functools.partial(factor_body, total), out_shape=(VMEM((sn...  8.87 us
    pallas_call x1, Pallas kernels, basis(): pl.pallas_call(functools.partial(basis_body, rows), out_shape=(jax.ShapeD...  8.77 us
    pallas_call x1, Pallas kernels, edges(): pl.pallas_call(functools.partial(edge_body, rows), out_shape=(packed, pac...  7.5 us
    pallas_call x1, Pallas kernels, partial_gram(): pl.pallas_call(functools.partial(gram_body, rows), out_shape=(halves, hal...  7.36 us
    ppermute x1, starting transfers between devices, on_device(): north = lax.ppermute(high, 'lat', [(i, i + 1) for i in range(lat - 1)])  4.99 us
  transfers between devices with their start and end apart: 12, of which 8 were waited for; matrix products, arithmetic and copies ran while one was open for 0% of the time, Pallas kernels for 23%

profile of v3, /device:TPU:0, one launch (start us, length us, event | category | flops | bytes accessed | tf_op | source)
XLA Modules:
  0.0 73.4 jit_solution(8474730540499072520)
XLA Ops:
  0.6 1.5 %rims.1 = (f32[4,256,128]{2,1,0:T(8,128)S(1)}, f32[4,256,128]{2,1,0:T(8,128)S(1)}) custom-call(f32[256,48,128]{2,1,0:T(8,128)} %u_ref.4, f32[256,48,128]{2,1,0:T(8,128)} %v_ref.4), custom_call_target="tpu_custom_call" | custom-call | bytes 4194304 | tf_op jit(solution)/shard_map/rims/pallas_call | solution.py:64
  2.1 5.0 %collective-permute-start.2 = (f32[4,256,128]{2,1,0:T(8,128)S(1)}, f32[4,256,128]{2,1,0:T(8,128)S(1)}, u32[]{:S(2)}, u32[]{:S(2)}) collective-permute-start(f32[4,256,128]{2,1,0:T(8,128)S(1)} %get-tuple-element.16), channel_id=1, source_target_pairs={{0,1},{1,2},{2,3},{4,5},{5,6},{6,7},{8,9},{9,10},{10,11},{12,13},{... | collective-permute-start | bytes 1572872 | tf_op jit(solution)/shard_map/ppermute | solution.py:644
  7.1 1.3 %collective-permute-start.3 = (f32[4,256,128]{2,1,0:T(8,128)S(1)}, f32[4,256,128]{2,1,0:T(8,128)S(1)}, u32[]{:S(2)}, u32[]{:S(2)}) collective-permute-start(f32[4,256,128]{2,1,0:T(8,128)S(1)} %get-tuple-element.15), channel_id=1, source_target_pairs={{1,0},{2,1},{3,2},{5,4},{6,5},{7,6},{9,8},{10,9},{11,10},{13,12},{... | collective-permute-start | bytes 1572872 | tf_op jit(solution)/shard_map/ppermute | solution.py:645
  8.4 7.5 %edges.1 = (f32[2,256,128]{2,1,0:T(8,128)S(1)}, f32[2,256,128]{2,1,0:T(8,128)S(1)}, f32[8,128]{1,0:T(8,128)S(1)}) custom-call(f32[256,48,128]{2,1,0:T(8,128)} %u_ref.4, f32[256,48,128]{2,1,0:T(8,128)} %v_ref.4, f32[4,8,128]{2,1,0:T(8,128)} %constant.25.clone.lanes_ref), custom_call_target="tpu_custom_call" | custom-call | flops 12582912 | bytes 12582912 | tf_op jit(solution)/shard_map/edges/pallas_call | solution.py:204
  15.9 0.1 collective-permute-start
  16.0 2.6 %collective-permute-start.1 = (f32[2,256,128]{2,1,0:T(8,128)S(1)}, f32[2,256,128]{2,1,0:T(8,128)S(1)}, u32[]{:S(2)}, u32[]{:S(2)}) collective-permute-start(f32[2,256,128]{2,1,0:T(8,128)S(1)} %get-tuple-element.19.west_ref), channel_id=1, source_target_pairs={{4,0},{8,4},{12,8},{16,12},{20,16},{24,20},{28,24},{0,28},{5,1},{9... | collective-permute-start | bytes 786440 | tf_op jit(solution)/shard_map/ppermute | solution.py:669
  18.6 9.7 %differences.1.x_ref = f32[44,256,256]{2,1,0:T(8,128)S(1)} custom-call(f32[256,48,128]{2,1,0:T(8,128)} %u_ref.4, f32[256,48,128]{2,1,0:T(8,128)} %v_ref.4, f32[4096]{0:T(1024)} %constant.24.clone.table_ref), custom_call_target="tpu_custom_call" | custom-call | flops 3221225472 | bytes 25165824 | tf_op jit(solution)/shard_map/differences/pallas_call | solution.py:261
  28.3 0.0 collective-permute-done.from_west_ref
  28.3 0.0 collective-permute-done.1.from_east_ref
  28.3 0.0 collective-permute-done.2.north_ref
  28.3 0.0 collective-permute-done.3.south_ref
  28.3 7.4 %partial_gram.1 = (bf16[48,256,256]{2,1,0:T(8,128)(2,1)S(1)}, bf16[48,256,256]{2,1,0:T(8,128)(2,1)S(1)}, f32[2,136,128]{2,1,0:T(8,128)S(1)}) custom-call(f32[44,256,256]{2,1,0:T(8,128)S(1)} %differences.1.x_ref, f32[2,256,128]{2,1,0:T(8,128)S(1)} %get-tuple-element.19.west_ref, f32[2,256,128]{2,1,0:T(8,128)S(1)} %get-tuple-element.20.east_ref, ...), custom_call_target="tpu_custom_call" | custom-call | flops 3221225472 | bytes 25165824 | tf_op jit(solution)/shard_map/partial_gram/pallas_call | solution.py:388
  35.7 0.1 collective-permute-start.4
  35.8 1.2 %collective-permute-done.4 = f32[136,128]{1,0:T(8,128)S(1)} collective-permute-done((f32[136,128]{1,0:T(8,128)S(1)}, f32[136,128]{1,0:T(8,128)S(1)}, u32[]{:S(2)}, u32[]{:S(2)}) %collective-permute-start.4) | collective-permute-done | bytes 69664 | tf_op jit(solution)/shard_map/ppermute | solution.py:417
  37.0 0.7 collective-permute-start.5
  37.7 1.5 %collective-permute-start.6 = (f32[136,128]{1,0:T(8,128)S(1)}, f32[136,128]{1,0:T(8,128)S(1)}, u32[]{:S(2)}, u32[]{:S(2)}) collective-permute-start(f32[136,128]{1,0:T(8,128)S(1)} %bitcast_add_fusion), channel_id=1, source_target_pairs={{0,16},{4,20},{8,24},{12,28},{16,0},{20,4},{24,8},{28,12},{1,17},{... | collective-permute-start | bytes 208904 | tf_op jit(solution)/shard_map/ppermute | solution.py:417
  39.2 1.4 %collective-permute-start.7 = (f32[136,128]{1,0:T(8,128)S(1)}, f32[136,128]{1,0:T(8,128)S(1)}, u32[]{:S(2)}, u32[]{:S(2)}) collective-permute-start(f32[136,128]{1,0:T(8,128)S(1)} %bitcast_add_fusion), channel_id=1, source_target_pairs={{0,24},{4,28},{8,16},{12,20},{16,8},{20,12},{24,0},{28,4},{1,25},{... | collective-permute-start | bytes 208904 | tf_op jit(solution)/shard_map/ppermute | solution.py:417
  40.6 0.9 %collective-permute-done.5 = f32[136,128]{1,0:T(8,128)S(1)} collective-permute-done((f32[136,128]{1,0:T(8,128)S(1)}, f32[136,128]{1,0:T(8,128)S(1)}, u32[]{:S(2)}, u32[]{:S(2)}) %collective-permute-start.5) | collective-permute-done | bytes 69664 | tf_op jit(solution)/shard_map/ppermute | solution.py:417
  41.5 0.5 collective-permute-done.6
  42.0 2.4 %collective-permute-done.7 = f32[136,128]{1,0:T(8,128)S(1)} collective-permute-done((f32[136,128]{1,0:T(8,128)S(1)}, f32[136,128]{1,0:T(8,128)S(1)}, u32[]{:S(2)}, u32[]{:S(2)}) %collective-permute-start.7) | collective-permute-done | bytes 69664 | tf_op jit(solution)/shard_map/ppermute | solution.py:417
  44.5 4.7 %collective-permute-start.10 = (f32[136,128]{1,0:T(8,128)S(1)}, f32[136,128]{1,0:T(8,128)S(1)}, u32[]{:S(2)}, u32[]{:S(2)}) collective-permute-start(f32[136,128]{1,0:T(8,128)S(1)} %add_add_fusion.1), channel_id=1, source_target_pairs={{0,3},{1,2},{2,1},{3,0},{4,7},{5,6},{6,5},{7,4},{8,11},{9,10},{10,... | collective-permute-start | bytes 208904 | tf_op jit(solution)/shard_map/ppermute | solution.py:417
  49.2 0.0 collective-permute-start.8
  49.2 0.6 collective-permute-start.9
  49.8 1.7 %collective-permute-done.10 = f32[136,128]{1,0:T(8,128)S(1)} collective-permute-done((f32[136,128]{1,0:T(8,128)S(1)}, f32[136,128]{1,0:T(8,128)S(1)}, u32[]{:S(2)}, u32[]{:S(2)}) %collective-permute-start.10) | collective-permute-done | bytes 69664 | tf_op jit(solution)/shard_map/ppermute | solution.py:417
  51.6 1.9 %collective-permute-done.8 = f32[136,128]{1,0:T(8,128)S(1)} collective-permute-done((f32[136,128]{1,0:T(8,128)S(1)}, f32[136,128]{1,0:T(8,128)S(1)}, u32[]{:S(2)}, u32[]{:S(2)}) %collective-permute-start.8) | collective-permute-done | bytes 69664 | tf_op jit(solution)/shard_map/ppermute | solution.py:417
  53.5 0.9 %collective-permute-done.9 = f32[136,128]{1,0:T(8,128)S(1)} collective-permute-done((f32[136,128]{1,0:T(8,128)S(1)}, f32[136,128]{1,0:T(8,128)S(1)}, u32[]{:S(2)}, u32[]{:S(2)}) %collective-permute-start.9) | collective-permute-done | bytes 69664 | tf_op jit(solution)/shard_map/ppermute | solution.py:417
  54.4 0.1 collective-permute-start.11
  54.5 1.2 %collective-permute-done.11 = f32[136,128]{1,0:T(8,128)S(1)} collective-permute-done((f32[136,128]{1,0:T(8,128)S(1)}, f32[136,128]{1,0:T(8,128)S(1)}, u32[]{:S(2)}, u32[]{:S(2)}) %collective-permute-start.11) | collective-permute-done | bytes 69664 | tf_op jit(solution)/shard_map/ppermute | solution.py:417
  55.8 8.9 %factor.1 = (f32[256,256]{1,0:T(8,128)S(1)}, bf16[256,256]{1,0:T(8,128)(2,1)S(1)}, bf16[256,256]{1,0:T(8,128)(2,1)S(1)}) custom-call(f32[136,128]{1,0:T(8,128)S(1)} %get-tuple-element.29.corner_ref, f32[136,128]{1,0:T(8,128)S(1)} %get-tuple-element.28.mixed_ref), custom_call_target="tpu_custom_call" | custom-call | flops 67108864 | bytes 1048576 | tf_op jit(solution)/shard_map/factor/pallas_call | solution.py:547
  64.6 8.8 %basis.1 = (f32[256,2,48,128]{3,2,1,0:T(8,128)}, f32[256,256]{1,0:T(8,128)}) custom-call(bf16[256,256]{1,0:T(8,128)(2,1)S(1)} %get-tuple-element.23.whi_ref, bf16[256,256]{1,0:T(8,128)(2,1)S(1)} %get-tuple-element.24.wlo_ref, bf16[48,256,256]{2,1,0:T(8,128)(2,1)S(1)} %get-tuple-element.25.hi_ref, bf16[48,256,256]{2,1,0:T(8,128)(2,1)S(1)} %get-tuple-element.26.lo_ref, ...), custom_call_target="tpu_custom_call" | custom-call | flops 4831838208 | bytes 25165824 | tf_op jit(solution)/shard_map/basis/pallas_call | solution.py:617
  (5 shorter events, 0.1 us)
Async XLA Ops:
  2.1 26.2 %collective-permute-start.2 = (f32[4,256,128]{2,1,0:T(8,128)S(1)}, f32[4,256,128]{2,1,0:T(8,128)S(1)}, u32[]{:S(2)}, u32[]{:S(2)}) collective-permute-start(f32[4,256,128]{2,1,0:T(8,128)S(1)} %get-tuple-element.16), channel_id=1, source_target_pairs={{0,1},{1,2},{2,3},{4,5},{5,6},{6,7},{8,9},{9,10},{10,11},{12,13},{... | collective-permute-start | bytes 1572872 | tf_op jit(solution)/shard_map/ppermute | solution.py:644
  7.1 21.2 %collective-permute-start.3 = (f32[4,256,128]{2,1,0:T(8,128)S(1)}, f32[4,256,128]{2,1,0:T(8,128)S(1)}, u32[]{:S(2)}, u32[]{:S(2)}) collective-permute-start(f32[4,256,128]{2,1,0:T(8,128)S(1)} %get-tuple-element.15), channel_id=1, source_target_pairs={{1,0},{2,1},{3,2},{5,4},{6,5},{7,6},{9,8},{10,9},{11,10},{13,12},{... | collective-permute-start | bytes 1572872 | tf_op jit(solution)/shard_map/ppermute | solution.py:645
  15.9 12.4 %collective-permute-start = (f32[2,256,128]{2,1,0:T(8,128)S(1)}, f32[2,256,128]{2,1,0:T(8,128)S(1)}, u32[]{:S(2)}, u32[]{:S(2)}) collective-permute-start(f32[2,256,128]{2,1,0:T(8,128)S(1)} %get-tuple-element.20.east_ref), channel_id=1, source_target_pairs={{0,4},{4,8},{8,12},{12,16},{16,20},{20,24},{24,28},{28,0},{1,5},{5... | collective-permute-start | bytes 786440 | tf_op jit(solution)/shard_map/ppermute | solution.py:668
  16.0 12.3 %collective-permute-start.1 = (f32[2,256,128]{2,1,0:T(8,128)S(1)}, f32[2,256,128]{2,1,0:T(8,128)S(1)}, u32[]{:S(2)}, u32[]{:S(2)}) collective-permute-start(f32[2,256,128]{2,1,0:T(8,128)S(1)} %get-tuple-element.19.west_ref), channel_id=1, source_target_pairs={{4,0},{8,4},{12,8},{16,12},{20,16},{24,20},{28,24},{0,28},{5,1},{9... | collective-permute-start | bytes 786440 | tf_op jit(solution)/shard_map/ppermute | solution.py:669
  35.7 1.3 %collective-permute-start.4 = (f32[136,128]{1,0:T(8,128)S(1)}, f32[136,128]{1,0:T(8,128)S(1)}, u32[]{:S(2)}, u32[]{:S(2)}) collective-permute-start(f32[136,128]{1,0:T(8,128)S(1)} %select_bitcast_fusion), channel_id=1, source_target_pairs={{0,4},{4,0},{8,12},{12,8},{16,20},{20,16},{24,28},{28,24},{1,5},{5... | collective-permute-start | bytes 208904 | tf_op jit(solution)/shard_map/ppermute | solution.py:417
  37.0 4.4 %collective-permute-start.5 = (f32[136,128]{1,0:T(8,128)S(1)}, f32[136,128]{1,0:T(8,128)S(1)}, u32[]{:S(2)}, u32[]{:S(2)}) collective-permute-start(f32[136,128]{1,0:T(8,128)S(1)} %bitcast_add_fusion), channel_id=1, source_target_pairs={{0,8},{4,12},{8,0},{12,4},{16,24},{20,28},{24,16},{28,20},{1,9},{5... | collective-permute-start | bytes 208904 | tf_op jit(solution)/shard_map/ppermute | solution.py:417
  37.7 4.3 %collective-permute-start.6 = (f32[136,128]{1,0:T(8,128)S(1)}, f32[136,128]{1,0:T(8,128)S(1)}, u32[]{:S(2)}, u32[]{:S(2)}) collective-permute-start(f32[136,128]{1,0:T(8,128)S(1)} %bitcast_add_fusion), channel_id=1, source_target_pairs={{0,16},{4,20},{8,24},{12,28},{16,0},{20,4},{24,8},{28,12},{1,17},{... | collective-permute-start | bytes 208904 | tf_op jit(solution)/shard_map/ppermute | solution.py:417
  39.2 5.2 %collective-permute-start.7 = (f32[136,128]{1,0:T(8,128)S(1)}, f32[136,128]{1,0:T(8,128)S(1)}, u32[]{:S(2)}, u32[]{:S(2)}) collective-permute-start(f32[136,128]{1,0:T(8,128)S(1)} %bitcast_add_fusion), channel_id=1, source_target_pairs={{0,24},{4,28},{8,16},{12,20},{16,8},{20,12},{24,0},{28,4},{1,25},{... | collective-permute-start | bytes 208904 | tf_op jit(solution)/shard_map/ppermute | solution.py:417
  44.5 7.1 %collective-permute-start.10 = (f32[136,128]{1,0:T(8,128)S(1)}, f32[136,128]{1,0:T(8,128)S(1)}, u32[]{:S(2)}, u32[]{:S(2)}) collective-permute-start(f32[136,128]{1,0:T(8,128)S(1)} %add_add_fusion.1), channel_id=1, source_target_pairs={{0,3},{1,2},{2,1},{3,0},{4,7},{5,6},{6,5},{7,4},{8,11},{9,10},{10,... | collective-permute-start | bytes 208904 | tf_op jit(solution)/shard_map/ppermute | solution.py:417
  49.2 4.3 %collective-permute-start.8 = (f32[136,128]{1,0:T(8,128)S(1)}, f32[136,128]{1,0:T(8,128)S(1)}, u32[]{:S(2)}, u32[]{:S(2)}) collective-permute-start(f32[136,128]{1,0:T(8,128)S(1)} %add_add_fusion.1), channel_id=1, source_target_pairs={{0,1},{1,0},{2,3},{3,2},{4,5},{5,4},{6,7},{7,6},{8,9},{9,8},{10,11... | collective-permute-start | bytes 208904 | tf_op jit(solution)/shard_map/ppermute | solution.py:417
  49.2 5.2 %collective-permute-start.9 = (f32[136,128]{1,0:T(8,128)S(1)}, f32[136,128]{1,0:T(8,128)S(1)}, u32[]{:S(2)}, u32[]{:S(2)}) collective-permute-start(f32[136,128]{1,0:T(8,128)S(1)} %add_add_fusion.1), channel_id=1, source_target_pairs={{0,2},{1,3},{2,0},{3,1},{4,6},{5,7},{6,4},{7,5},{8,10},{9,11},{10,... | collective-permute-start | bytes 208904 | tf_op jit(solution)/shard_map/ppermute | solution.py:417
  54.4 1.3 %collective-permute-start.11 = (f32[136,128]{1,0:T(8,128)S(1)}, f32[136,128]{1,0:T(8,128)S(1)}, u32[]{:S(2)}, u32[]{:S(2)}) collective-permute-start(f32[136,128]{1,0:T(8,128)S(1)} %add_add_fusion), channel_id=1, source_target_pairs={{0,4},{4,0},{8,12},{12,8},{16,20},{20,16},{24,28},{28,24},{1,5},{5... | collective-permute-start | bytes 208904 | tf_op jit(solution)/shard_map/ppermute | solution.py:417
